TPU v7x, 32 devices: a whole 2x2x4 slice. The times are simulated.
32 devices in a mesh: dp: 2 (over x), ctx: 4 (over y, core), tp: 4 (over z).
Axes of the slice: x: 2, y: 2, z: 4, core: 2. Of those that a mesh axis runs over, the one named last changes fastest.
Arguments:
- tokens: bfloat16 [2, 4096, 768], P('dp', 'ctx'), may hold values from -6 to 6
- time_steps: int32 [2], P('dp'), may hold values from 0 to 999
- lengths: int32 [2], P('dp'), may hold values from 2048 to 4096, as said below
- time_table: bfloat16 [1000, 768], P(None, 'dp'), may hold values from -3 to 3
- norm_gains: bfloat16 [2, 768], P(None, 'dp'), may hold values from 0.5 to 1.5
- norm_biases: bfloat16 [2, 768], P(None, 'dp'), may hold values from -1 to 1
- w_qkv: bfloat16 [3, 768, 768], P(None, 'dp', 'tp'), may hold values from -0.3125 to 0.3125
- b_qv: bfloat16 [2, 768], P(None, 'tp'), may hold values from -0.099609375 to 0.099609375
- w_out: bfloat16 [768, 768], P('tp', 'dp'), may hold values from -0.3125 to 0.3125
- out_biases: bfloat16 [2, 768], P(None, 'dp'), may hold values from -1.25 to 1.25
- w_up: bfloat16 [768, 3072], P('dp', 'tp'), may hold values from -0.21875 to 0.21875
- b_up: bfloat16 [3072], P('tp'), may hold values from -1 to 1
- w_down: bfloat16 [3072, 768], P('tp', 'dp'), may hold values from -0.109375 to 0.109375
- cotangent: bfloat16 [2, 4096, 768], P('dp', 'ctx'), may hold values from -6 to 6
Outputs:
- layer_out: bfloat16 [2, 4096, 768], P('dp', 'ctx')
- grad_tokens: float32 [2, 4096, 768], P('dp', 'ctx')
- grad_time_table: float32 [1000, 768], P(None, 'dp')
- grad_norm_gains: float32 [2, 768], P(None, 'dp')
- grad_norm_biases: float32 [2, 768], P(None, 'dp')
- grad_w_qkv: float32 [3, 768, 768], P(None, 'dp', 'tp')
- grad_b_qv: float32 [2, 768], P(None, 'tp')
- grad_w_out: float32 [768, 768], P('tp', 'dp')
- grad_out_biases: float32 [2, 768], P(None, 'dp')
- grad_w_up: float32 [768, 3072], P('dp', 'tp')
- grad_b_up: float32 [3072], P('tp')
- grad_w_down: float32 [3072, 768], P('tp', 'dp')
Inputs may be any that keep to these rules, and one draw needn't show every extreme that they name: `lengths`: every sequence has 2048 to 4096 real tokens at its start, the rest padding; some sequence has exactly 4096.
All inputs are finite; a program needn't handle non-finite values.
Results may differ from a plain program's by a relative error of at most 0.019.
Values may be sent and summed in bfloat16 or wider, within the bound.
No kernel may reach another device: no remote copies, remote signals or barrier semaphores. Data moves between devices by JAX's collectives and lax.ppermute only.
A program may use at most 128 MiB of HBM per device.

v0:
```python
import functools

import jax
import jax.numpy as jnp
from jax import lax
from jax.experimental import pallas as pl
from jax.experimental.pallas import tpu as pltpu
from jax.sharding import PartitionSpec as P

HEAD = 64
norm_eps = 1e-05
NT = (((1,), (1,)), ((), ()))
NN = (((1,), (0,)), ((), ()))
f32 = jnp.float32
bf16 = jnp.bfloat16
KERNEL_VMEM = 60 * 2**20


def dot(a, b, dims=NN):
    return lax.dot_general(a, b, dims, preferred_element_type=f32)


def attend_body(heads, piece, blocks, first, last, q_ref, *refs):
    kv_refs, bias_refs, refs = refs[:blocks], refs[blocks : 2 * blocks], refs[2 * blocks :]
    if not first:
        (part_ref, old_ref), refs = refs[:2], refs[2:]
    out_ref, stat_ref, score_ref = refs[0], refs[1], refs[-1]
    rows = q_ref.shape[0]
    length = kv_refs[0].shape[1]
    width = heads * HEAD
    pieces = [(b, c) for b in range(blocks) for c in range(0, length, piece)]
    stats = []
    for h in range(heads):
        cols = slice(h * HEAD, (h + 1) * HEAD)
        vals = slice(width + h * HEAD, width + (h + 1) * HEAD)
        q = q_ref[:, cols]
        peak = None
        for b, c in pieces:
            scores = dot(q, kv_refs[b][cols, c : c + piece]) + bias_refs[b][:, c : c + piece]
            score_ref[h, :, b * length + c : b * length + c + piece] = scores
            for j in range(0, piece, 128):
                part = scores[:, j : j + 128]
                peak = part if peak is None else jnp.maximum(peak, part)
        peak = jnp.max(peak, axis=1, keepdims=True)
        if not first:
            old_peak = old_ref[:, h : h + 1]
            peak = jnp.maximum(peak, old_peak)
        total, summed = None, None
        for b, c in pieces:
            weights = jnp.exp(score_ref[h, :, b * length + c : b * length + c + piece] - peak)
            for j in range(0, piece, 128):
                part = weights[:, j : j + 128]
                total = part if total is None else total + part
            part = dot(weights.astype(bf16), kv_refs[b][vals, c : c + piece], NT)
            summed = part if summed is None else summed + part
        total = jnp.sum(total, axis=1, keepdims=True)
        if not first:
            shrink = jnp.exp(old_peak - peak)
            total = total + old_ref[:, 8 + h : 9 + h] * shrink
            summed = summed + part_ref[:, cols] * shrink
        if last:
            summed = summed / total
        stats.append((peak, total))
        out_ref[:, cols] = summed
        if last:
            refs[2][:, cols] = summed.astype(bf16)
    lane = lax.broadcasted_iota(jnp.int32, (rows, 128), 1)
    packed = jnp.zeros((rows, 128), f32)
    for h, (peak, total) in enumerate(stats):
        if last:
            packed = jnp.where(lane == h, peak + jnp.log(total), packed)
        else:
            packed = jnp.where(lane == h, peak, packed)
            packed = jnp.where(lane == 8 + h, total, packed)
    stat_ref[...] = packed


def row_spec(rows, width):
    return pl.BlockSpec((rows, width), lambda i: (i, 0))


def whole_spec(array):
    zeros = (0,) * array.ndim
    return pl.BlockSpec(array.shape, lambda i: zeros)


def attend(queries, kvs, biases, carry, last, rows=128, piece=512):
    count, width = queries.shape
    length = kvs[0].shape[1]
    heads = width // HEAD
    keys = length * len(kvs)
    args = [queries, *kvs, *biases]
    specs = [row_spec(rows, width)] + [whole_spec(a) for a in args[1:]]
    if carry is not None:
        args += list(carry)
        specs += [row_spec(rows, width), row_spec(rows, 128)]
    return pl.pallas_call(
        functools.partial(attend_body, heads, piece, len(kvs), carry is None, last),
        grid=(count // rows,),
        in_specs=specs,
        out_specs=[row_spec(rows, width), row_spec(rows, 128)]
        + [row_spec(rows, width)] * last,
        out_shape=[
            jax.ShapeDtypeStruct((count, width), f32),
            jax.ShapeDtypeStruct((count, 128), f32),
        ]
        + [jax.ShapeDtypeStruct((count, width), bf16)] * last,
        scratch_shapes=[pltpu.VMEM((heads, rows, keys), f32)],
        cost_estimate=pl.CostEstimate(
            flops=16 * count * keys * width,
            bytes_accessed=count * width * 6 + keys * width * 4,
            transcendentals=count * keys * heads,
        ),
        compiler_params=pltpu.CompilerParams(vmem_limit_bytes=KERNEL_VMEM),
        name="attend",
    )(*args)


def attend_back_body(heads, piece, blocks, first, q_ref, do_ref, att_ref, log_ref, *refs):
    kv_refs, bias_refs, refs = refs[:blocks], refs[blocks : 2 * blocks], refs[2 * blocks :]
    if not first:
        part_ref, refs = refs[0], refs[1:]
    dq_ref, dkv_refs, sum_refs = refs[0], refs[1 : 1 + blocks], refs[1 + blocks :]
    step = pl.program_id(0)
    length = kv_refs[0].shape[1]
    width = heads * HEAD

    @pl.when(step == 0)
    def _():
        for sum_ref in sum_refs:
            sum_ref[...] = jnp.zeros_like(sum_ref)

    q, do = q_ref[...], do_ref[...]
    q_t, do_t = q.T, do.T
    product = do.astype(f32) * att_ref[...]
    for h in range(heads):
        cols = slice(h * HEAD, (h + 1) * HEAD)
        vals = slice(width + h * HEAD, width + (h + 1) * HEAD)
        delta = jnp.sum(product[:, cols], axis=1, keepdims=True)
        log_total = log_ref[:, h : h + 1]
        dq = None
        for b in range(blocks):
            for c in range(0, length, piece):
                span = slice(c, c + piece)
                scores = dot(q[:, cols], kv_refs[b][cols, span]) + bias_refs[b][:, span]
                probs = jnp.exp(scores - log_total)
                grads = dot(do[:, cols], kv_refs[b][vals, span])
                score_grad = (probs * (grads - delta)).astype(bf16)
                part = dot(score_grad, kv_refs[b][cols, span], NT)
                dq = part if dq is None else dq + part
                sum_refs[b][cols, span] += dot(q_t[cols, :], score_grad)
                sum_refs[b][vals, span] += dot(do_t[cols, :], probs.astype(bf16))
        dq = dq * HEAD ** (-0.5)
        if not first:
            dq = dq + part_ref[:, cols]
        dq_ref[:, cols] = dq.astype(dq_ref.dtype)

    @pl.when(step == pl.num_programs(0) - 1)
    def _():
        for dkv_ref, sum_ref in zip(dkv_refs, sum_refs):
            dkv_ref[...] = sum_ref[...].astype(dkv_ref.dtype)


def attend_back(queries, do, att, log_total, kvs, biases, part, rows=256, piece=1024):
    count, width = queries.shape
    length = kvs[0].shape[1]
    heads = width // HEAD
    keys = length * len(kvs)
    args = [queries, do, att, log_total, *kvs, *biases]
    specs = [row_spec(rows, width)] * 3 + [row_spec(rows, 128)]
    specs += [whole_spec(a) for a in args[4:]]
    if part is not None:
        args.append(part)
        specs.append(row_spec(rows, width))
    return pl.pallas_call(
        functools.partial(attend_back_body, heads, piece, len(kvs), part is None),
        grid=(count // rows,),
        in_specs=specs,
        out_specs=[row_spec(rows, width)] + [whole_spec(kv) for kv in kvs],
        out_shape=[jax.ShapeDtypeStruct((count, width), f32 if part is None else bf16)]
        + [jax.ShapeDtypeStruct(kv.shape, bf16) for kv in kvs],
        scratch_shapes=[pltpu.VMEM(kv.shape, f32) for kv in kvs],
        cost_estimate=pl.CostEstimate(
            flops=4 * count * keys * width,
            bytes_accessed=count * width * 12 + keys * width * 8,
            transcendentals=count * keys * heads,
        ),
        compiler_params=pltpu.CompilerParams(vmem_limit_bytes=KERNEL_VMEM),
        name="attend_back",
    )(*args)


def middle_body(
    num_ref, att_ref, tok_ref, emb_ref, par_ref, cot_ref, wout_ref, w_ref,
    layer_ref, back_ref, do_ref, keep_ref, send_ref, keepo_ref, sendo_ref, vec_ref, bvec_ref,
    mid_ref, sec_ref, sect_ref, upl_ref, uplt_ref, mlp_ref, sback_ref,
):
    step = pl.program_id(0)
    tps, rows, width = att_ref.shape
    model = tok_ref.shape[1]
    wide = w_ref.shape[2] // 2
    blocks, sub = keep_ref.shape[0], keep_ref.shape[2]
    low_core = num_ref[3] == 0

    def store(keep, send, left, right, t, at):
        half = right.shape[1] // 2
        low, high = right[:, :half], right[:, half:]
        for ref, chosen in (
            (keep, jnp.where(low_core, low, high)),
            (send, jnp.where(low_core, high, low)),
        ):
            value = dot(left, chosen)
            for b in range(blocks):
                ref[b, t, :, at : at + half] = value[b * sub : (b + 1) * sub].astype(bf16)

    @pl.when(step == 0)
    def _():
        start = tok_ref[...].astype(f32) + emb_ref[...]
        attn = None
        for t in range(tps):
            part = dot(att_ref[t], wout_ref[t][:, :width], NT)
            attn = part if attn is None else attn + part
        middle = start + attn + par_ref[2:3, :]
        mid_ref[...] = middle
        center = middle - jnp.mean(middle, axis=1, keepdims=True)
        scale = lax.rsqrt(jnp.mean(center * center, axis=1, keepdims=True) + norm_eps)
        second = (center * scale * par_ref[0:1, :] + par_ref[1:2, :]).astype(bf16)
        sec_ref[...] = second
        sect_ref[...] = second.T
        place = num_ref[0] + lax.broadcasted_iota(jnp.int32, (rows, model), 0)
        upstream = jnp.where(place < num_ref[1], cot_ref[...].astype(f32), 0.0)
        low = upstream.astype(bf16)
        upl_ref[...] = low
        uplt_ref[...] = low.T
        mlp_ref[...] = jnp.zeros_like(mlp_ref)
        sback_ref[...] = jnp.zeros_like(sback_ref)

    w_up, w_down = w_ref[0, :, :wide], w_ref[0, :, wide:]
    b_up = wout_ref[step][:, width:].astype(f32).T[0:1, :]
    hidden = dot(sec_ref[...], w_up) + b_up
    half = 0.5 * (1.0 + lax.erf(hidden * (0.5**0.5)))
    activated = (hidden * half).astype(bf16)
    mlp_ref[...] += dot(activated, w_down, NT)
    act_back = dot(upl_ref[...], w_down)
    slope = half + hidden * (jnp.exp(-0.5 * hidden * hidden) * 0.3989422804014327)
    hidden_back = (act_back * slope).astype(bf16)
    sback_ref[...] += dot(hidden_back, w_up, NT)
    bvec_ref[pl.ds(step, 1), :] = jnp.sum(hidden_back.astype(f32), axis=0, keepdims=True)
    store(keep_ref, send_ref, sect_ref[...], hidden_back, 0, 0)
    store(keep_ref, send_ref, uplt_ref[...], activated, 0, wide // 2)

    @pl.when(step == pl.num_programs(0) - 1)
    def _():
        middle = mid_ref[...]
        layer_ref[...] = (middle + mlp_ref[...] + par_ref[3:4, :]).astype(bf16)
        center = middle - jnp.mean(middle, axis=1, keepdims=True)
        scale = lax.rsqrt(jnp.mean(center * center, axis=1, keepdims=True) + norm_eps)
        n = center * scale
        e = sback_ref[...]
        eg = e * par_ref[0:1, :]
        norm = scale * (
            eg
            - jnp.mean(eg, axis=1, keepdims=True)
            - n * jnp.mean(eg * n, axis=1, keepdims=True)
        )
        upstream = upl_ref[...].astype(f32)
        back = upstream + norm
        back_ref[...] = back
        low = back.astype(bf16)
        low_t = low.T
        keepo_ref[...] = jnp.zeros_like(keepo_ref)
        sendo_ref[...] = jnp.zeros_like(sendo_ref)
        for t in range(tps):
            do_ref[t] = dot(low, wout_ref[t][:, :width]).astype(bf16)
            store(keepo_ref, sendo_ref, low_t, att_ref[t], t, 0)
        vec_ref[0:1, :] = jnp.sum(e * n, axis=0, keepdims=True)
        vec_ref[1:2, :] = jnp.sum(e, axis=0, keepdims=True)
        vec_ref[2:3, :] = jnp.sum(low.astype(f32), axis=0, keepdims=True)
        vec_ref[3:4, :] = jnp.sum(upstream, axis=0, keepdims=True)
        vec_ref[4:8, :] = jnp.zeros((4, model), f32)


def middle_part(numbers, att, tokens, embedded, params, cotangent, weights, wide, blocks):
    tps, rows, width = att.shape
    model = tokens.shape[1]
    packed = weights.shape[2]
    fixed = lambda shape: pl.BlockSpec(shape, lambda i, n: (0,) * len(shape))
    mine = pl.BlockSpec((rows, model), lambda i, n: (n[2], 0))
    spare = packed - 2 * wide
    sub = model // blocks
    small = (blocks, tps, sub, 128)
    moving = pl.BlockSpec((blocks, 1, sub, wide), lambda i, n: (0, i, 0, 0))
    return pl.pallas_call(
        middle_body,
        grid_spec=pltpu.PrefetchScalarGridSpec(
            num_scalar_prefetch=1,
            grid=(tps,),
            in_specs=[
                fixed(att.shape),
                mine,
                fixed(embedded.shape),
                fixed(params.shape),
                mine,
                pl.BlockSpec((tps, model, spare), lambda i, n: (0, 0, 2 * wide // spare)),
                pl.BlockSpec((1, model, 2 * wide), lambda i, n: (i, 0, 0)),
            ],
            out_specs=[
                fixed((rows, model)),
                fixed((rows, model)),
                fixed(att.shape),
                moving,
                moving,
                fixed(small),
                fixed(small),
                fixed((8, model)),
                fixed((tps, wide)),
            ],
            scratch_shapes=[
                pltpu.VMEM((rows, model), f32),
                pltpu.VMEM((rows, model), bf16),
                pltpu.VMEM((model, rows), bf16),
                pltpu.VMEM((rows, model), bf16),
                pltpu.VMEM((model, rows), bf16),
                pltpu.VMEM((rows, model), f32),
                pltpu.VMEM((rows, model), f32),
            ],
        ),
        out_shape=[
            jax.ShapeDtypeStruct((rows, model), bf16),
            jax.ShapeDtypeStruct((rows, model), f32),
            jax.ShapeDtypeStruct(att.shape, bf16),
            jax.ShapeDtypeStruct((blocks, tps, sub, wide), bf16),
            jax.ShapeDtypeStruct((blocks, tps, sub, wide), bf16),
            jax.ShapeDtypeStruct(small, bf16),
            jax.ShapeDtypeStruct(small, bf16),
            jax.ShapeDtypeStruct((8, model), f32),
            jax.ShapeDtypeStruct((tps, wide), f32),
        ],
        cost_estimate=pl.CostEstimate(
            flops=12 * rows * model * wide * tps,
            bytes_accessed=2 * weights.size * 2,
            transcendentals=2 * rows * wide * tps,
        ),
        compiler_params=pltpu.CompilerParams(vmem_limit_bytes=KERNEL_VMEM),
        name="middle",
    )(numbers, att, tokens, embedded, params, cotangent, weights, weights)


def flip(value, axis, bit=1, size=2):
    return lax.ppermute(value, axis, [(i, i ^ bit) for i in range(size)])


def after(value, *others):
    return lax.optimization_barrier((value, *others))[0]


def swap_rows(value):
    return lax.all_to_all(value, "tp", 0, 0, tiled=True)


def gather_dp(value, dps, axis):
    if dps != 2:
        return lax.all_gather(value, "dp", axis=axis, tiled=True)
    return pair(value, "dp", axis)


def pair(value, axis_name, axis):
    other = flip(value, axis_name)
    first = lax.axis_index(axis_name) == 0
    return jnp.concatenate(
        (jnp.where(first, value, other), jnp.where(first, other, value)), axis=axis
    )


def add_low(*terms):
    total = terms[0].astype(f32)
    for term in terms[1:]:
        total = total + term.astype(f32)
    return total.astype(bf16)


def sum_vectors(value, dps, tps, then):
    for axis in ("core", "y"):
        value = value + flip(value, axis)
    value = after(value, then)
    if dps == 2:
        value = value + flip(value, "dp")
    else:
        value = lax.psum(value, "dp")
    for bit in (1, 2):
        value = value + flip(value, "tp", bit, tps)
    return value


def reduce_projections(grad, dps):
    if dps != 2:
        grad = lax.psum_scatter(grad, ("dp", "y", "core"), scatter_dimension=0, tiled=True)
        return lax.all_gather(grad, ("y", "core"), axis=0, tiled=True)
    dp, y, core = lax.axis_index("dp"), lax.axis_index("y"), lax.axis_index("core")
    size = grad.shape[0] // 8
    grad = grad.reshape(2, 2, 2 * size, -1)
    pick = lambda v, i, axis: lax.dynamic_index_in_dim(v, i, axis, False)
    grad = add_low(pick(grad, core, 1), flip(pick(grad, 1 - core, 1), "core"))
    grad = add_low(pick(grad, dp, 0), flip(pick(grad, 1 - dp, 0), "dp"))
    grad = grad.reshape(2, size, -1)
    grad = add_low(pick(grad, y, 0), flip(pick(grad, 1 - y, 0), "y"))
    return pair(pair(grad, "y", 0), "core", 0)


def join_body(keep_ref, send_ref, keepo_ref, sendo_ref, out_ref):
    wide = keep_ref.shape[-1]
    for t in range(keep_ref.shape[1]):
        total = keep_ref[0, t].astype(f32) + send_ref[0, t].astype(f32)
        out_ref[0, t, :, :wide] = total.astype(bf16)
        total = keepo_ref[0, t].astype(f32) + sendo_ref[0, t].astype(f32)
        out_ref[0, t, :, wide:] = total.astype(bf16)


def join(keep, send, keep_o, send_o):
    blocks, tps, sub, wide = keep.shape
    spec = lambda last: pl.BlockSpec((1, tps, sub, last), lambda i: (i, 0, 0, 0))
    return pl.pallas_call(
        join_body,
        grid=(blocks,),
        in_specs=[spec(wide), spec(wide), spec(128), spec(128)],
        out_specs=spec(wide + 128),
        out_shape=jax.ShapeDtypeStruct((blocks, tps, sub, wide + 128), bf16),
        cost_estimate=pl.CostEstimate(
            flops=keep.size, bytes_accessed=7 * keep.size, transcendentals=0
        ),
        name="join",
    )(keep, send, keep_o, send_o)


def unpack_body(half, half_out, core_ref, mine_ref, other_ref, up_ref, down_ref, out_ref):
    low_core = core_ref[0] == 0
    mine, other = mine_ref[...].astype(f32), other_ref[...].astype(f32)
    halves = (jnp.where(low_core, mine, other), jnp.where(low_core, other, mine))
    for i, value in enumerate(halves):
        up_ref[:, i * half : (i + 1) * half] = value[:, :half]
        down_ref[i * half : (i + 1) * half, :] = value[:, half : 2 * half].T
        turned = value[:, 2 * half :].T
        out_ref[i * half_out : (i + 1) * half_out, :] = turned[:half_out]


def unpack(mine, other, core, half, half_out):
    part = mine.shape[0]
    shapes = ((part, 2 * half), (2 * half, part), (2 * half_out, part))
    if part % 128:
        first = core == 0
        halves = (jnp.where(first, mine, other), jnp.where(first, other, mine))
        pick = lambda a, b: jnp.concatenate([h[:, a:b] for h in halves], axis=1).astype(f32)
        return (
            pick(0, half),
            pick(half, 2 * half).T,
            pick(2 * half, 2 * half + half_out).T,
        )
    fixed = lambda shape: pl.BlockSpec(shape, lambda i, n: (0,) * len(shape))
    return pl.pallas_call(
        functools.partial(unpack_body, half, half_out),
        grid_spec=pltpu.PrefetchScalarGridSpec(
            num_scalar_prefetch=1,
            grid=(1,),
            in_specs=[fixed(mine.shape)] * 2,
            out_specs=[fixed(shape) for shape in shapes],
        ),
        out_shape=[jax.ShapeDtypeStruct(shape, f32) for shape in shapes],
        name="unpack",
    )(core[None].astype(jnp.int32), mine, other)


def spread_rows(value, tps):
    copies = swap_rows(jnp.broadcast_to(value[None], (tps, *value.shape)))
    return copies.reshape(tps * value.shape[0], value.shape[1])


def on_device(
    dps, tps,
    tokens, time_steps, lengths, time_table, norm_gains, norm_biases, w_qkv, b_qv, w_out,
    out_biases, w_up, b_up, w_down, cotangent,
):
    _, row_count, model = tokens.shape
    local = b_qv.shape[1]
    wide = b_up.shape[0]
    part = w_up.shape[0]
    steps_in_table = time_table.shape[0]
    rows = row_count // tps
    dp, tp = lax.axis_index("dp"), lax.axis_index("tp")
    core = lax.axis_index("core")
    ctx = 2 * lax.axis_index("y") + core

    all_steps = gather_dp(time_steps, dps, 0)
    small = jnp.concatenate((norm_gains, norm_biases, out_biases, time_table[all_steps]))
    small = gather_dp(small, dps, 1).astype(f32)
    embedded = lax.dynamic_slice_in_dim(small, 6 + dp, 1, 0)
    gain_first, shift_first = small[0:1], small[2:3]
    params = jnp.stack(
        (small[1], small[3], small[4], small[5], small[1], small[1], small[1], small[1])
    )

    qkv_mine = jnp.concatenate((w_qkv[0], w_qkv[1], w_qkv[2]), axis=1)
    qkv_full = gather_dp(qkv_mine, dps, 0)
    slab = part // 4
    spare = -(-(local + 1) // 128) * 128
    piece = jnp.concatenate(
        (
            lax.dynamic_slice_in_dim(w_up, ctx * slab, slab, 0),
            lax.dynamic_slice_in_dim(w_down, ctx * slab, slab, 1).T,
            lax.dynamic_slice_in_dim(w_out, ctx * slab, slab, 1).T,
            lax.dynamic_slice_in_dim(b_up, dp * part + ctx * slab, slab, 0)[:, None],
            jnp.zeros((slab, spare - local - 1), bf16),
        ),
        axis=1,
    )
    weights = lax.all_gather(piece, ("tp", "dp", "y", "core"), axis=0, tiled=True)
    weights = weights.reshape(tps, model, 2 * wide + spare)

    flat = tokens.reshape(row_count, model)
    start = flat.astype(f32) + embedded
    center = start - jnp.mean(start, axis=1, keepdims=True)
    scale = lax.rsqrt(jnp.mean(center * center, axis=1, keepdims=True) + norm_eps)
    normed = (center * scale * gain_first + shift_first).astype(bf16)
    bias = b_qv.astype(f32)
    kv_bias = jnp.concatenate((jnp.zeros((local,), f32), bias[1]))[:, None]
    kv = lax.dot_general(
        qkv_full[:, local:], normed, (((0,), (1,)), ((), ())), preferred_element_type=f32
    )
    kv = (kv + kv_bias).astype(bf16)
    queries = (dot(normed, qkv_full[:, :local]) + bias[0]).astype(bf16) * bf16(HEAD**-0.5)

    place = jnp.arange(row_count)[None, :]

    def key_bias(owner):
        return jnp.where(owner * row_count + place < lengths[0], 0.0, -1e30).astype(f32)

    biases = [key_bias(ctx ^ b) for b in range(4)]
    kv_1 = flip(kv, "core")
    kv_2 = flip(kv, "y")
    carry = attend(queries, (kv, kv_1), biases[:2], None, False)
    kv_2 = after(kv_2, *carry)
    kv_3 = flip(kv_2, "core")
    attended, log_total, attended_low = attend(queries, (kv_2, kv_3), biases[2:], carry, True)

    swapped = swap_rows(attended_low.reshape(tps, rows, local))
    numbers = jnp.stack((ctx * row_count + tp * rows, lengths[0], tp, core)).astype(jnp.int32)
    layer_rows, middle_back, output_back, keep, send, keep_o, send_o, vectors, grad_b_up = middle_part(
        numbers,
        swapped,
        flat,
        embedded,
        params,
        cotangent.reshape(row_count, model),
        weights,
        wide,
        2 * dps,
    )
    output_back = swap_rows(output_back).reshape(row_count, local)

    send, send_o, output_back = lax.optimization_barrier(
        (flip(send, "core"), flip(send_o, "core"), output_back)
    )
    grad_packed = join(keep, send, keep_o, send_o)
    output_back = after(output_back, grad_packed)
    grad_packed = grad_packed.reshape(2 * dps * tps * part // 2, -1)
    grad_packed = lax.psum_scatter(grad_packed, ("dp", "y"), scatter_dimension=0, tiled=True)
    grad_packed = lax.psum_scatter(grad_packed, "tp", scatter_dimension=0, tiled=True)

    layer_out = spread_rows(after(layer_rows, output_back), tps)
    dq, dkv_2, dkv_3 = attend_back(
        queries, output_back, attended, log_total, (kv_2, kv_3), biases[2:], None
    )
    far = add_low(dkv_2, flip(dkv_3, "core"))
    dq = after(dq, far)
    far = flip(far, "y")
    dq, dkv_0, dkv_1 = attend_back(
        queries, output_back, attended, log_total, (kv, kv_1), biases[:2], dq
    )
    dkv_1, layer_out = lax.optimization_barrier((dkv_1, layer_out))
    near = flip(dkv_1, "core")
    dkv = add_low(dkv_0, near, far)

    back = dot(dq, qkv_full[:, :local], NT) + lax.dot_general(
        dkv, qkv_full[:, local:], (((0,), (1,)), ((), ())), preferred_element_type=f32
    )
    back = swap_rows(back.astype(bf16).reshape(tps, rows, model))
    grad_qkv = jnp.concatenate(
        (
            lax.dot_general(normed, dq, (((0,), (0,)), ((), ())), preferred_element_type=f32),
            lax.dot_general(normed, dkv, (((0,), (1,)), ((), ())), preferred_element_type=f32),
        ),
        axis=1,
    ).astype(bf16)
    grad_qkv = reduce_projections(grad_qkv, dps).astype(f32)
    grad_w_qkv = jnp.stack([grad_qkv[:, i * local : (i + 1) * local] for i in range(3)])

    e = jnp.sum(back.astype(f32), axis=0)
    mine = lax.dynamic_slice_in_dim(flat, tp * rows, rows, 0).astype(f32) + embedded
    center = mine - jnp.mean(mine, axis=1, keepdims=True)
    scale = lax.rsqrt(jnp.mean(center * center, axis=1, keepdims=True) + norm_eps)
    n = center * scale
    eg = e * gain_first
    start_norm = scale * (
        eg - jnp.mean(eg, axis=1, keepdims=True) - n * jnp.mean(eg * n, axis=1, keepdims=True)
    )
    grad_rows = middle_back + start_norm
    grad_tokens = spread_rows(grad_rows.astype(bf16), tps).astype(f32)

    token_sums = jnp.zeros((dps, model), f32)
    token_sums = lax.dynamic_update_slice_in_dim(
        token_sums, jnp.sum(grad_rows, axis=0, keepdims=True), dp, 0
    )
    qv_sums = jnp.concatenate(
        (jnp.sum(dq.astype(f32), axis=0), jnp.sum(dkv[local:].astype(f32), axis=1))
    )
    qv_slots = jnp.zeros((tps, 2 * local), f32)
    qv_slots = lax.dynamic_update_slice_in_dim(qv_slots, qv_sums[None], tp, 0)
    sums = jnp.concatenate(
        (
            vectors[:4],
            jnp.sum(e * n, axis=0, keepdims=True),
            jnp.sum(e, axis=0, keepdims=True),
            token_sums,
            grad_b_up.reshape(-1, model),
            qv_slots.reshape(-1, model),
        )
    )
    sums = after(sums, grad_packed)
    grad_packed = pair(grad_packed, "y", 0)
    grad_other = flip(grad_packed, "core")
    grad_w_up, grad_w_down, grad_w_out = unpack(
        grad_packed, grad_other, core, wide // 2, local // 2
    )
    sums = sum_vectors(sums, dps, tps, grad_other)
    own = lax.dynamic_slice_in_dim(sums, dp * part, part, 1)
    grad_gains = jnp.stack((own[4], own[0]))
    grad_shifts = jnp.stack((own[5], own[1]))
    grad_out_biases = jnp.stack((own[2], own[3]))
    at = 6 + dps
    b_rows = grad_b_up.size // model
    grad_b_up = lax.dynamic_slice_in_dim(
        sums[at : at + b_rows].reshape(-1), tp * wide, wide, 0
    )
    grad_b_qv = lax.dynamic_index_in_dim(
        sums[at + b_rows :].reshape(tps, 2, local), tp, 0, False
    )
    step_rows = jnp.arange(steps_in_table)[:, None]
    grad_table = jnp.zeros((steps_in_table, part), f32)
    for s in range(dps):
        grad_table = grad_table + jnp.where(step_rows == all_steps[s], own[6 + s][None], 0.0)
    return (
        layer_out[None],
        grad_tokens[None],
        grad_table,
        grad_gains,
        grad_shifts,
        grad_w_qkv,
        grad_b_qv,
        grad_w_out,
        grad_out_biases,
        grad_w_up,
        grad_b_up,
        grad_w_down,
    )


def solution(mesh):
    in_specs = (
        P("dp", ("y", "core"), None),
        P("dp"),
        P("dp"),
        P(None, "dp"),
        P(None, "dp"),
        P(None, "dp"),
        P(None, "dp", "tp"),
        P(None, "tp"),
        P("tp", "dp"),
        P(None, "dp"),
        P("dp", "tp"),
        P("tp"),
        P("tp", "dp"),
        P("dp", ("y", "core"), None),
    )
    out_specs = (
        P("dp", ("y", "core"), None),
        P("dp", ("y", "core"), None),
        P(None, "dp"),
        P(None, "dp"),
        P(None, "dp"),
        P(None, "dp", "tp"),
        P(None, "tp"),
        P("tp", "dp"),
        P(None, "dp"),
        P("dp", "tp"),
        P("tp"),
        P("tp", "dp"),
    )
    sizes = (mesh.shape["dp"], mesh.shape["tp"])
    fine = jax.sharding.Mesh(
        mesh.devices.reshape(sizes[0], 2, mesh.shape["ctx"] // 2, sizes[1]),
        ("dp", "y", "core", "tp"),
    )
    return jax.shard_map(
        functools.partial(on_device, *sizes),
        mesh=fine,
        in_specs=in_specs,
        out_specs=out_specs,
        check_vma=False,
    )
```

profile of v0, /device:TPU:0, one launch (start us, length us, event | category | flops | bytes accessed | tf_op | source)
XLA Modules:
  0.0 350.6 jit_solution(4827640439539211880)
XLA Ops:
  8.3 1.1 constant_dynamic-slice_fusion.5
  10.5 1.0 constant_dynamic-slice_fusion.4
  12.5 3.0 collective-permute-start
  19.1 2.1 collective-permute-start.1
  21.3 7.8 %collective-permute-done.1 = bf16[8,384]{1,0:T(8,128)(2,1)S(1)} collective-permute-done((bf16[8,384]{1,0:T(8,128)(2,1)S(1)}, bf16[8,384]{1,0:T(8,128)(2,1)S(1)}, u32[]{:S(2)}, u32[]{:S(2)}) %collective-permute-start.1) | collective-permute-done | bytes 6176 | tf_op jit(solution)/shard_map/ppermute | solution.py:350
  31.7 1.5 broadcast_select_fusion.1
  35.5 1.2 collective-permute-start.3
  36.6 2.8 fusion.3.q_ref
  40.3 16.1 %attend.2 = (f32[1024,192]{1,0:T(8,128)}, f32[1024,128]{1,0:T(8,128)}) custom-call(bf16[1024,192]{1,0:T(8,128)(2,1)} %fusion.3.q_ref, bf16[384,1024]{1,0:T(8,128)(2,1)} %copy-done.28, bf16[384,1024]{1,0:T(8,128)(2,1)} %copy-done.29, f32[1,1024]{1,0:T(1,128)} %get-tuple-element.126.refs_2_, f32[1,1024]{1,0:T(1,128)} %get-tuple-element.125.refs_3_), custom_call_target="tpu_custom_call" | custom-call | flops 6442450944 | bytes 2752512 | tf_op jit(solution)/shard_map/attend/pallas_call | solution.py:97
  56.4 4.0 %collective-permute-done.3.refs_0_ = bf16[384,1024]{1,0:T(8,128)(2,1)} collective-permute-done((bf16[384,1024]{1,0:T(8,128)(2,1)S(1)}, bf16[384,1024]{1,0:T(8,128)(2,1)}, u32[]{:S(2)}, u32[]{:S(2)}) %collective-permute-start.3) | collective-permute-done | bytes 786464 | tf_op jit(solution)/shard_map/ppermute | solution.py:350
  61.0 1.9 collective-permute-done.5.refs_1_
  63.8 20.3 %attend.3 = (f32[1024,192]{1,0:T(8,128)}, f32[1024,128]{1,0:T(8,128)}, bf16[1024,192]{1,0:T(8,128)(2,1)}) custom-call(bf16[1024,192]{1,0:T(8,128)(2,1)} %fusion.3.q_ref, bf16[384,1024]{1,0:T(8,128)(2,1)} %collective-permute-done.3.refs_0_, bf16[384,1024]{1,0:T(8,128)(2,1)} %copy-done.30, f32[1,1024]{1,0:T(1,128)} %get-tuple-element.124.refs_2_, ...), custom_call_target="tpu_custom_call" | custom-call | flops 6442450944 | bytes 2752512 | tf_op jit(solution)/shard_map/attend/pallas_call | solution.py:97
  84.0 2.0 copy.42
  86.0 5.5 %all-to-all-start = ((bf16[4,256,192]{1,2,0:T(8,128)(2,1)}), bf16[4,256,192]{1,2,0:T(8,128)(2,1)S(1)}, u32[]{:S(2)}, u32[]{:S(2)}) async-start(bf16[4,256,192]{1,2,0:T(8,128)(2,1)} %copy.42), calls=%async_computation | async-start | bytes 786432 | tf_op jit(solution)/shard_map/all_to_all | solution.py:358
  92.8 19.3 %all-to-all-done = bf16[4,256,192]{1,2,0:T(8,128)(2,1)S(1)} async-done(((bf16[4,256,192]{1,2,0:T(8,128)(2,1)}), bf16[4,256,192]{1,2,0:T(8,128)(2,1)S(1)}, u32[]{:S(2)}, u32[]{:S(2)}) %all-to-all-start) | async-done | bytes 393248 | tf_op jit(solution)/shard_map/all_to_all | solution.py:358
  112.1 1.0 copy.46.att_ref
  113.1 1.4 all-gather.2.cloned.1.call-done
  114.6 18.8 %middle.1 = (bf16[256,768]{1,0:T(8,128)(2,1)}, f32[256,768]{1,0:T(8,128)}, bf16[4,256,192]{2,1,0:T(8,128)(2,1)}, bf16[4,4,192,768]{3,2,1,0:T(8,128)(2,1)}, bf16[...) custom-call(s32[4]{0:T(128)} %pad_add_fusion.num_ref, ...), custom_call_target="tpu_custom_call" | custom-call | flops 7247757312 | bytes 22020096 | tf_op jit(solution)/shard_map/middle/pallas_call | solution.py:293
  133.9 1.2 copy.47
  135.2 14.8 %all_to_all.25 = bf16[4,256,192]{1,2,0:T(8,128)(2,1)S(1)} all-to-all(bf16[4,256,192]{1,2,0:T(8,128)(2,1)S(1)} %copy.47), channel_id=1, replica_groups=mesh['dp'=2,'y'=2,'core'=2,'tp'=4] {'tp'}, dimensions={0} | all-to-all | bytes 786432 | tf_op jit(solution)/shard_map/all_to_all | solution.py:358
  149.9 1.0 copy.48
  151.8 7.1 %join.1 = bf16[4,4,192,896]{3,2,1,0:T(8,128)(2,1)} custom-call(bf16[4,4,192,768]{3,2,1,0:T(8,128)(2,1)} %get-tuple-element.54.keep_ref, bf16[4,4,192,768]{3,2,1,0:T(8,128)(2,1)} %collective-permute-done.6.send_ref, bf16[4,4,192,128]{3,2,1,0:T(8,128)(2,1)} %get-tuple-element.56.keepo_ref, bf16[4,4,192,128]{3,2,1,0:T(8,128)(2,1)} %copy-done.15), custom_call_target="tpu_custom_call" | custom-call | flops 2359296 | bytes 16515072 | tf_op jit(solution)/shard_map/join/pallas_call | solution.py:422
  159.9 1.2 broadcast_in_dim.105
  161.2 3.9 %all-to-all-start.2 = ((bf16[4,256,768]{2,1,0:T(8,128)(2,1)}), bf16[4,256,768]{2,1,0:T(8,128)(2,1)S(1)}, u32[]{:S(2)}, u32[]{:S(2)}) async-start(bf16[4,256,768]{2,1,0:T(8,128)(2,1)} %broadcast_in_dim.105), calls=%async_computation.2 | async-start | bytes 3145728 | tf_op jit(solution)/shard_map/all_to_all | solution.py:358
  165.1 20.4 %attend_back.2 = (f32[1024,192]{1,0:T(8,128)}, bf16[384,1024]{1,0:T(8,128)(2,1)}, bf16[384,1024]{1,0:T(8,128)(2,1)}) custom-call(bf16[1024,192]{1,0:T(8,128)(2,1)} %fusion.3.q_ref, bf16[1024,192]{1,0:T(8,128)(2,1)} %bitcast.102, f32[1024,192]{1,0:T(8,128)} %get-tuple-element.59.att_ref, f32[1024,128]{1,0:T(8,128)} %get-tuple-element.60.log_ref, ...), custom_call_target="tpu_custom_call" | custom-call | flops 1610612736 | bytes 5505024 | tf_op jit(solution)/shard_map/attend_back/pallas_call | solution.py:175
  185.6 2.5 collective-permute-done.8
  188.1 2.3 add_convert_fusion.3
  190.4 1.4 collective-permute-start.10
  191.8 20.7 %attend_back.3 = (bf16[1024,192]{1,0:T(8,128)(2,1)}, bf16[384,1024]{1,0:T(8,128)(2,1)}, bf16[384,1024]{1,0:T(8,128)(2,1)}) custom-call(bf16[1024,192]{1,0:T(8,128)(2,1)} %fusion.3.q_ref, bf16[1024,192]{1,0:T(8,128)(2,1)} %bitcast.103, f32[1024,192]{1,0:T(8,128)} %get-tuple-element.59.att_ref, f32[1024,128]{1,0:T(8,128)} %get-tuple-element.60.log_ref, ...), custom_call_target="tpu_custom_call" | custom-call | flops 1610612736 | bytes 5505024 | tf_op jit(solution)/shard_map/attend_back/pallas_call | solution.py:175
  212.6 5.7 %collective-permute-done.10 = bf16[384,1024]{1,0:T(8,128)(2,1)S(1)} collective-permute-done((bf16[384,1024]{1,0:T(8,128)(2,1)}, bf16[384,1024]{1,0:T(8,128)(2,1)S(1)}, u32[]{:S(2)}, u32[]{:S(2)}) %collective-permute-start.10) | collective-permute-done | bytes 786464 | tf_op jit(solution)/shard_map/ppermute | solution.py:350
  219.2 1.8 add_convert_fusion.2
  221.0 1.0 fusion.26
  222.1 1.7 add_convert_fusion
  223.8 4.7 %all-to-all-start.3 = ((bf16[4,256,768]{2,1,0:T(8,128)(2,1)}), bf16[4,256,768]{2,1,0:T(8,128)(2,1)}, u32[]{:S(2)}, u32[]{:S(2)}) async-start(bf16[4,256,768]{2,1,0:T(8,128)(2,1)} %bitcast.97), calls=%async_computation.3 | async-start | bytes 3145728 | tf_op jit(solution)/shard_map/all_to_all | solution.py:358
  228.6 1.9 fusion.42
  230.5 2.7 copy.49
  233.2 2.1 convolution_convert_fusion.1
  235.3 1.0 convolution_convert_fusion
  236.3 1.0 fusion.21
  237.8 1.8 collective-permute-done.18
  239.5 1.3 fusion.4
  240.9 1.5 collective-permute-start.19
  242.4 6.5 %collective-permute-done.19 = bf16[192,576]{1,0:T(8,128)(2,1)S(1)} collective-permute-done((bf16[192,576]{1,0:T(8,128)(2,1)S(1)}, bf16[192,576]{1,0:T(8,128)(2,1)S(1)}, u32[]{:S(2)}, u32[]{:S(2)}) %collective-permute-start.19) | collective-permute-done | bytes 221216 | tf_op jit(solution)/shard_map/ppermute | solution.py:350
  249.7 37.3 %all-to-all-done.3 = bf16[4,256,768]{2,1,0:T(8,128)(2,1)} async-done(((bf16[4,256,768]{2,1,0:T(8,128)(2,1)}), bf16[4,256,768]{2,1,0:T(8,128)(2,1)}, u32[]{:S(2)}, u32[]{:S(2)}) %all-to-all-start.3) | async-done | bytes 1572896 | tf_op jit(solution)/shard_map/all_to_all | solution.py:358
  287.0 2.2 convert_reduce_fusion
  290.0 1.2 broadcast_in_dim.107
  291.2 3.7 %all-to-all-start.4 = ((bf16[4,256,768]{2,1,0:T(8,128)(2,1)}), bf16[4,256,768]{2,1,0:T(8,128)(2,1)S(1)}, u32[]{:S(2)}, u32[]{:S(2)}) async-start(bf16[4,256,768]{2,1,0:T(8,128)(2,1)} %broadcast_in_dim.107), calls=%async_computation.4 | async-start | bytes 3145728 | tf_op jit(solution)/shard_map/all_to_all | solution.py:358
  296.0 6.5 %collective-permute-done.20 = bf16[96,576]{0,1:T(8,128)(2,1)S(1)} collective-permute-done((bf16[96,576]{0,1:T(8,128)(2,1)}, bf16[96,576]{0,1:T(8,128)(2,1)S(1)}, u32[]{:S(2)}, u32[]{:S(2)}) %collective-permute-start.20) | collective-permute-done | bytes 110624 | tf_op jit(solution)/shard_map/ppermute | solution.py:350
  302.6 2.0 collective-permute-start.13
  304.7 3.2 collective-permute-done.21
  308.0 3.6 %collective-permute-done.13 = bf16[192,896]{1,0:T(8,128)(2,1)S(1)} collective-permute-done((bf16[192,896]{1,0:T(8,128)(2,1)}, bf16[192,896]{1,0:T(8,128)(2,1)S(1)}, u32[]{:S(2)}, u32[]{:S(2)}) %collective-permute-start.13) | collective-permute-done | bytes 344096 | tf_op jit(solution)/shard_map/ppermute | solution.py:350
  311.7 1.0 broadcast_select_fusion.3
  314.7 1.0 collective-permute-done.22
  315.8 1.2 broadcast_select_fusion.5
  317.7 3.5 %collective-permute-done.12 = f32[14,768]{1,0:T(8,128)S(1)} collective-permute-done((f32[14,768]{1,0:T(8,128)S(1)}, f32[14,768]{1,0:T(8,128)S(1)}, u32[]{:S(2)}, u32[]{:S(2)}) %collective-permute-start.12) | collective-permute-done | bytes 43040 | tf_op jit(solution)/shard_map/ppermute | solution.py:350
  321.2 1.5 collective-permute-start.15
  322.8 2.6 collective-permute-done.15
  325.4 2.0 collective-permute-start.16
  328.4 2.1 collective-permute-done.16
  330.5 2.0 collective-permute-start.17
  332.5 1.9 bitcast_convert_fusion
  334.4 3.2 unpack.1
  340.9 1.5 select_add_fusion
  342.4 1.1 copy.65
  (174 shorter events, 26.9 us)
Async XLA Ops:
  7.2 11.3 %copy-start = (bf16[1000,384]{1,0:T(8,128)(2,1)S(1)}, bf16[1000,384]{1,0:T(8,128)(2,1)}, u32[]{:S(2)}) copy-start(bf16[1000,384]{1,0:T(8,128)(2,1)} %param.17) | copy-start | bytes 2304004
  7.2 8.3 %copy-start.18 = (bf16[3,384,192]{1,2,0:T(8,128)(2,1)S(1)}, bf16[3,384,192]{1,2,0:T(8,128)(2,1)}, u32[]{:S(2)}) copy-start(bf16[3,384,192]{1,2,0:T(8,128)(2,1)} %param.20) | copy-start | bytes 1327108
  7.2 107.4 %all-gather.2.cloned.1.call-start = ((), (), s32[]{:S(2)}) async-start(), calls=%async_computation.7 | async-start | bytes 11354112 | tf_op jit(solution)/shard_map/all_gather | solution.py:515
  10.5 8.6 %copy-start.23 = (bf16[2,384]{1,0:T(2,128)(2,1)S(1)}, bf16[2,384]{1,0:T(2,128)(2,1)}, u32[]{:S(2)}) copy-start(bf16[2,384]{1,0:T(2,128)(2,1)} %param.23) | copy-start | bytes 4612
  10.5 8.6 %copy-start.24 = (bf16[2,384]{1,0:T(2,128)(2,1)S(1)}, bf16[2,384]{1,0:T(2,128)(2,1)}, u32[]{:S(2)}) copy-start(bf16[2,384]{1,0:T(2,128)(2,1)} %param.19) | copy-start | bytes 4612
  10.5 8.6 %copy-start.25 = (bf16[2,384]{1,0:T(2,128)(2,1)S(1)}, bf16[2,384]{1,0:T(2,128)(2,1)}, u32[]{:S(2)}) copy-start(bf16[2,384]{1,0:T(2,128)(2,1)} %param.18) | copy-start | bytes 4612
  10.5 10.7 %copy-start.27 = (bf16[2,192]{1,0:T(2,128)(2,1)S(1)}, bf16[2,192]{1,0:T(2,128)(2,1)}, u32[]{:S(2)}) copy-start(bf16[2,192]{1,0:T(2,128)(2,1)} %param.21) | copy-start | bytes 2308
  11.5 18.2 %copy-start.2 = (bf16[1,1024,768]{2,1,0:T(8,128)(2,1)S(1)}, bf16[1,1024,768]{2,1,0:T(8,128)(2,1)}, u32[]{:S(2)}) copy-start(bf16[1,1024,768]{2,1,0:T(8,128)(2,1)} %param.14) | copy-start | bytes 4718596
  12.5 4.7 %collective-permute-start = (s32[1]{0:T(128)}, s32[1]{0:T(128)}, u32[]{:S(2)}, u32[]{:S(2)}) collective-permute-start(s32[1]{0:T(128)} %param.15), channel_id=1, source_target_pairs={{0,16},{16,0},{1,17},{17,1},{2,18},{18,2},{3,19},{19,3},{4,20},{20... | collective-permute-start | bytes 20 | tf_op jit(solution)/shard_map/ppermute | solution.py:350
  15.6 15.2 %copy-start.12 = (bf16[384,192]{0,1:T(8,128)(2,1)}, bf16[384,192]{0,1:T(8,128)(2,1)S(1)}, u32[]{:S(2)}) copy-start(bf16[384,192]{0,1:T(8,128)(2,1)S(1)} %get-tuple-element.104) | copy-start | bytes 442372
  15.6 15.9 %collective-permute-start.2 = (bf16[384,576]{0,1:T(8,128)(2,1)S(1)}, bf16[384,576]{0,1:T(8,128)(2,1)}, u32[]{:S(2)}, u32[]{:S(2)}) collective-permute-start(bf16[384,576]{0,1:T(8,128)(2,1)S(1)} %pad_maximum_fusion.3), channel_id=1, source_target_pairs={{0,16},{16,0},{1,17},{17,1},{2,18},{18,2},{3,19},{19,3},{4,20},{20... | collective-permute-start | bytes 1327112 | tf_op jit(solution)/shard_map/ppermute | solution.py:350
  19.1 10.0 %collective-permute-start.1 = (bf16[8,384]{1,0:T(8,128)(2,1)S(1)}, bf16[8,384]{1,0:T(8,128)(2,1)S(1)}, u32[]{:S(2)}, u32[]{:S(2)}) collective-permute-start(bf16[8,384]{1,0:T(8,128)(2,1)S(1)} %pad_maximum_fusion.8), channel_id=1, source_target_pairs={{0,16},{16,0},{1,17},{17,1},{2,18},{18,2},{3,19},{19,3},{4,20},{20... | collective-permute-start | bytes 18440 | tf_op jit(solution)/shard_map/ppermute | solution.py:350
  30.8 0.7 copy-start.20
  30.8 0.9 copy-start.13
  31.5 2.5 copy-start.9
  34.1 5.3 %copy-start.28 = (bf16[384,1024]{1,0:T(8,128)(2,1)}, bf16[384,1024]{1,0:T(8,128)(2,1)S(1)}, u32[]{:S(2)}) copy-start(bf16[384,1024]{1,0:T(8,128)(2,1)S(1)} %add_convert_fusion.4.refs_0_) | copy-start | bytes 2359300
  34.1 5.3 %collective-permute-start.4 = (bf16[384,1024]{1,0:T(8,128)(2,1)S(1)}, bf16[384,1024]{1,0:T(8,128)(2,1)S(1)}, u32[]{:S(2)}, u32[]{:S(2)}) collective-permute-start(bf16[384,1024]{1,0:T(8,128)(2,1)S(1)} %add_convert_fusion.4.refs_0_), channel_id=1, source_target_pairs={{0,4},{4,0},{1,5},{5,1},{2,6},{6,2},{3,7},{7,3},{8,12},{12,8},{9,1... | collective-permute-start | bytes 2359304 | tf_op jit(solution)/shard_map/ppermute | solution.py:350
  35.5 24.9 %collective-permute-start.3 = (bf16[384,1024]{1,0:T(8,128)(2,1)S(1)}, bf16[384,1024]{1,0:T(8,128)(2,1)}, u32[]{:S(2)}, u32[]{:S(2)}) collective-permute-start(bf16[384,1024]{1,0:T(8,128)(2,1)S(1)} %add_convert_fusion.4.refs_0_), channel_id=1, source_target_pairs={{0,8},{8,0},{1,9},{9,1},{2,10},{10,2},{3,11},{11,3},{4,12},{12,4},... | collective-permute-start | bytes 2359304 | tf_op jit(solution)/shard_map/ppermute | solution.py:350
  39.4 0.9 copy-start.29
  60.4 2.5 collective-permute-start.5
  62.9 0.9 copy-start.30
  86.0 26.1 %all-to-all-start = ((bf16[4,256,192]{1,2,0:T(8,128)(2,1)}), bf16[4,256,192]{1,2,0:T(8,128)(2,1)S(1)}, u32[]{:S(2)}, u32[]{:S(2)}) async-start(bf16[4,256,192]{1,2,0:T(8,128)(2,1)} %copy.42), calls=%async_computation | async-start | bytes 786432 | tf_op jit(solution)/shard_map/all_to_all | solution.py:358
  91.5 146.0 %reduce-scatter.3.cloned.1.call-start = ((), (), s32[]{:S(2)}) async-start(), calls=%async_computation.8 | async-start | bytes 6881280 | tf_op jit(solution)/shard_map/reduce_scatter | solution.py:565
  133.3 17.6 %collective-permute-start.6 = (bf16[4,4,192,768]{3,2,1,0:T(8,128)(2,1)}, bf16[4,4,192,768]{3,2,1,0:T(8,128)(2,1)}, u32[]{:S(2)}, u32[]{:S(2)}) collective-permute-start(bf16[4,4,192,768]{3,2,1,0:T(8,128)(2,1)} %get-tuple-element.50), channel_id=1, source_target_pairs={{0,4},{4,0},{1,5},{5,1},{2,6},{6,2},{3,7},{7,3},{8,12},{12,8},{9,1... | collective-permute-start | bytes 14155784 | tf_op jit(solution)/shard_map/ppermute | solution.py:350
  133.7 17.3 %collective-permute-start.7 = (bf16[4,4,192,128]{3,2,1,0:T(8,128)(2,1)}, bf16[4,4,192,128]{3,2,1,0:T(8,128)(2,1)S(1)}, u32[]{:S(2)}, u32[]{:S(2)}) collective-permute-start(bf16[4,4,192,128]{3,2,1,0:T(8,128)(2,1)} %get-tuple-element.51), channel_id=1, source_target_pairs={{0,4},{4,0},{1,5},{5,1},{2,6},{6,2},{3,7},{7,3},{8,12},{12,8},{9,1... | collective-permute-start | bytes 2359304 | tf_op jit(solution)/shard_map/ppermute | solution.py:350
  151.0 0.9 copy-start.15
  158.9 1.0 copy-start.19
  161.2 51.3 %all-to-all-start.2 = ((bf16[4,256,768]{2,1,0:T(8,128)(2,1)}), bf16[4,256,768]{2,1,0:T(8,128)(2,1)S(1)}, u32[]{:S(2)}, u32[]{:S(2)}) async-start(bf16[4,256,768]{2,1,0:T(8,128)(2,1)} %broadcast_in_dim.105), calls=%async_computation.2 | async-start | bytes 3145728 | tf_op jit(solution)/shard_map/all_to_all | solution.py:358
  185.5 2.6 collective-permute-start.8
  190.4 27.9 %collective-permute-start.10 = (bf16[384,1024]{1,0:T(8,128)(2,1)}, bf16[384,1024]{1,0:T(8,128)(2,1)S(1)}, u32[]{:S(2)}, u32[]{:S(2)}) collective-permute-start(bf16[384,1024]{1,0:T(8,128)(2,1)} %add_convert_fusion.3), channel_id=1, source_target_pairs={{0,8},{8,0},{1,9},{9,1},{2,10},{10,2},{3,11},{11,3},{4,12},{12,4},... | collective-permute-start | bytes 2359304 | tf_op jit(solution)/shard_map/ppermute | solution.py:350
  212.5 8.5 %copy-start.4 = (bf16[4,256,768]{2,1,0:T(8,128)(2,1)}, bf16[4,256,768]{2,1,0:T(8,128)(2,1)S(1)}, u32[]{:S(2)}) copy-start(bf16[4,256,768]{2,1,0:T(8,128)(2,1)S(1)} %all-to-all-done.2) | copy-start | bytes 4718596
  212.5 5.8 %collective-permute-start.9 = (bf16[384,1024]{1,0:T(8,128)(2,1)}, bf16[384,1024]{1,0:T(8,128)(2,1)S(1)}, u32[]{:S(2)}, u32[]{:S(2)}) collective-permute-start(bf16[384,1024]{1,0:T(8,128)(2,1)} %get-tuple-element.72), channel_id=1, source_target_pairs={{0,4},{4,0},{1,5},{5,1},{2,6},{6,2},{3,7},{7,3},{8,12},{12,8},{9,1... | collective-permute-start | bytes 2359304 | tf_op jit(solution)/shard_map/ppermute | solution.py:350
  218.3 0.9 copy-start.17
  221.0 1.0 copy-start.7
  223.8 4.8 %copy-start.3 = (bf16[1,1024,768]{2,1,0:T(8,128)(2,1)S(1)}, bf16[1,1024,768]{2,1,0:T(8,128)(2,1)}, u32[]{:S(2)}) copy-start(bf16[1,1024,768]{2,1,0:T(8,128)(2,1)} %param.14) | copy-start | bytes 4718596
  223.8 4.8 %copy-start.21 = (f32[1024]{0:T(1024)S(1)}, f32[1024]{0:T(1024)}, u32[]{:S(2)}) copy-start(f32[1024]{0:T(1024)} %copy-done.20) | copy-start | bytes 12292
  223.8 63.2 %all-to-all-start.3 = ((bf16[4,256,768]{2,1,0:T(8,128)(2,1)}), bf16[4,256,768]{2,1,0:T(8,128)(2,1)}, u32[]{:S(2)}, u32[]{:S(2)}) async-start(bf16[4,256,768]{2,1,0:T(8,128)(2,1)} %bitcast.97), calls=%async_computation.3 | async-start | bytes 3145728 | tf_op jit(solution)/shard_map/all_to_all | solution.py:358
  228.5 74.1 %reduce-scatter.5.cloned.1.call-start = ((), (), s32[]{:S(2)}) async-start(), calls=%async_computation.9 | async-start | bytes 1720320 | tf_op jit(solution)/shard_map/reduce_scatter | solution.py:566
  230.5 2.7 copy-start.8
  233.2 2.1 copy-start.10
  235.3 1.0 copy-start.11
  237.3 2.2 collective-permute-start.18
  240.9 8.1 %collective-permute-start.19 = (bf16[192,576]{1,0:T(8,128)(2,1)S(1)}, bf16[192,576]{1,0:T(8,128)(2,1)S(1)}, u32[]{:S(2)}, u32[]{:S(2)}) collective-permute-start(bf16[192,576]{1,0:T(8,128)(2,1)S(1)} %dynamic-slice_bitcast_fusion), channel_id=1, source_target_pairs={{0,16},{16,0},{1,17},{17,1},{2,18},{18,2},{3,19},{19,3},{4,20},{20... | collective-permute-start | bytes 663560 | tf_op jit(solution)/shard_map/ppermute | solution.py:350
  287.0 2.6 copy-start.16
  291.2 3.7 %copy-start.14 = (bf16[192,576]{1,0:T(8,128)(2,1)S(1)}, bf16[192,576]{1,0:T(8,128)(2,1)}, u32[]{:S(2)}) copy-start(bf16[192,576]{1,0:T(8,128)(2,1)} %fusion.24) | copy-start | bytes 663556
  291.2 4.6 %copy-start.26 = (f32[8,768]{1,0:T(8,128)S(1)}, f32[8,768]{1,0:T(8,128)}, u32[]{:S(2)}) copy-start(f32[8,768]{1,0:T(8,128)} %get-tuple-element.73) | copy-start | bytes 73732
  291.2 41.2 %all-to-all-start.4 = ((bf16[4,256,768]{2,1,0:T(8,128)(2,1)}), bf16[4,256,768]{2,1,0:T(8,128)(2,1)S(1)}, u32[]{:S(2)}, u32[]{:S(2)}) async-start(bf16[4,256,768]{2,1,0:T(8,128)(2,1)} %broadcast_in_dim.107), calls=%async_computation.4 | async-start | bytes 3145728 | tf_op jit(solution)/shard_map/all_to_all | solution.py:358
  295.8 6.7 %collective-permute-start.20 = (bf16[96,576]{0,1:T(8,128)(2,1)}, bf16[96,576]{0,1:T(8,128)(2,1)S(1)}, u32[]{:S(2)}, u32[]{:S(2)}) collective-permute-start(bf16[96,576]{0,1:T(8,128)(2,1)} %bitcast.40), channel_id=1, source_target_pairs={{0,8},{8,0},{1,9},{9,1},{2,10},{10,2},{3,11},{11,3},{4,12},{12,4},... | collective-permute-start | bytes 331784 | tf_op jit(solution)/shard_map/ppermute | solution.py:350
  302.5 5.5 %collective-permute-start.21 = (bf16[96,576]{0,1:T(8,128)(2,1)S(1)}, bf16[96,576]{0,1:T(8,128)(2,1)S(1)}, u32[]{:S(2)}, u32[]{:S(2)}) collective-permute-start(bf16[96,576]{0,1:T(8,128)(2,1)S(1)} %fusion.25), channel_id=1, source_target_pairs={{0,8},{8,0},{1,9},{9,1},{2,10},{10,2},{3,11},{11,3},{4,12},{12,4},... | collective-permute-start | bytes 331784 | tf_op jit(solution)/shard_map/ppermute | solution.py:350
  302.6 9.1 %collective-permute-start.13 = (bf16[192,896]{1,0:T(8,128)(2,1)}, bf16[192,896]{1,0:T(8,128)(2,1)S(1)}, u32[]{:S(2)}, u32[]{:S(2)}) collective-permute-start(bf16[192,896]{1,0:T(8,128)(2,1)} %reduce-scatter.5.cloned.1.call-done), channel_id=1, source_target_pairs={{0,8},{8,0},{1,9},{9,1},{2,10},{10,2},{3,11},{11,3},{4,12},{12,4},... | collective-permute-start | bytes 1032200 | tf_op jit(solution)/shard_map/ppermute | solution.py:350
  308.0 6.6 %copy-start.22 = (f32[4,768]{1,0:T(4,128)S(1)}, f32[4,768]{1,0:T(4,128)}, u32[]{:S(2)}) copy-start(f32[4,768]{1,0:T(4,128)} %get-tuple-element.74) | copy-start | bytes 36868
  312.8 4.9 %copy-start.6 = (bf16[384,896]{1,0:T(8,128)(2,1)}, bf16[384,896]{1,0:T(8,128)(2,1)S(1)}, u32[]{:S(2)}) copy-start(bf16[384,896]{1,0:T(8,128)(2,1)S(1)} %pad_maximum_fusion.1.mine_ref) | copy-start | bytes 2064388
  312.8 8.4 %collective-permute-start.14 = (bf16[384,896]{1,0:T(8,128)(2,1)S(1)}, bf16[384,896]{1,0:T(8,128)(2,1)}, u32[]{:S(2)}, u32[]{:S(2)}) collective-permute-start(bf16[384,896]{1,0:T(8,128)(2,1)S(1)} %pad_maximum_fusion.1.mine_ref), channel_id=1, source_target_pairs={{0,4},{4,0},{1,5},{5,1},{2,6},{6,2},{3,7},{7,3},{8,12},{12,8},{9,1... | collective-permute-start | bytes 2064392 | tf_op jit(solution)/shard_map/ppermute | solution.py:350
  313.7 2.0 collective-permute-start.22
  314.7 2.4 collective-permute-start.11
  317.1 4.2 %collective-permute-start.12 = (f32[14,768]{1,0:T(8,128)S(1)}, f32[14,768]{1,0:T(8,128)S(1)}, u32[]{:S(2)}, u32[]{:S(2)}) collective-permute-start(f32[14,768]{1,0:T(8,128)S(1)} %add.283), channel_id=1, source_target_pairs={{0,8},{8,0},{1,9},{9,1},{2,10},{10,2},{3,11},{11,3},{4,12},{12,4},... | collective-permute-start | bytes 129032 | tf_op jit(solution)/shard_map/ppermute | solution.py:350
  321.2 4.2 %collective-permute-start.15 = (f32[14,768]{1,0:T(8,128)S(1)}, f32[14,768]{1,0:T(8,128)S(1)}, u32[]{:S(2)}, u32[]{:S(2)}) collective-permute-start(f32[14,768]{1,0:T(8,128)S(1)} %add.284), channel_id=1, source_target_pairs={{0,16},{16,0},{1,17},{17,1},{2,18},{18,2},{3,19},{19,3},{4,20},{20... | collective-permute-start | bytes 129032 | tf_op jit(solution)/shard_map/ppermute | solution.py:350
  325.4 5.1 %collective-permute-start.16 = (f32[14,768]{1,0:T(8,128)S(1)}, f32[14,768]{1,0:T(8,128)S(1)}, u32[]{:S(2)}, u32[]{:S(2)}) collective-permute-start(f32[14,768]{1,0:T(8,128)S(1)} %add.285), channel_id=1, source_target_pairs={{0,1},{1,0},{2,3},{3,2},{4,5},{5,4},{6,7},{7,6},{8,9},{9,8},{10,11... | collective-permute-start | bytes 129032 | tf_op jit(solution)/shard_map/ppermute | solution.py:350
  330.5 7.1 %collective-permute-start.17 = (f32[14,768]{1,0:T(8,128)S(1)}, f32[14,768]{1,0:T(8,128)S(1)}, u32[]{:S(2)}, u32[]{:S(2)}) collective-permute-start(f32[14,768]{1,0:T(8,128)S(1)} %add.286), channel_id=1, source_target_pairs={{0,2},{1,3},{2,0},{3,1},{4,6},{5,7},{6,4},{7,5},{8,10},{9,11},{10,... | collective-permute-start | bytes 129032 | tf_op jit(solution)/shard_map/ppermute | solution.py:350
  334.4 8.0 %copy-start.5 = (bf16[4,256,768]{2,1,0:T(8,128)(2,1)S(1)}, bf16[4,256,768]{2,1,0:T(8,128)(2,1)}, u32[]{:S(2)}) copy-start(bf16[4,256,768]{2,1,0:T(8,128)(2,1)} %copy-done.4) | copy-start | bytes 4718596
  342.4 1.6 copy-start.1
Sparse Core Ops, SparseCore 0:
  12.6 101.9 all-gather.1
  159.1 69.4 reduce-scatter.2
  237.6 48.0 reduce-scatter.4
where the time goes:
time: 352 us; the launch traced here: 351 us
  waiting for transfers between devices  112 us (32%)
  Pallas kernels  107 us (30%)
  starting transfers between devices  36.6 us (10%)
  local copies, waits for them, and re-layouts  27.3 us (8%)
  other arithmetic  27 us (8%)
  between operations  17.1 us (5%)
  blocking collectives  14.8 us (4%)
  matrix products  9.44 us (3%)
    all_to_all x4, waiting for transfers between devices, swap_rows(): return lax.all_to_all(value, 'tp', 0, 0, tiled=True)  56.6 us
    ppermute x23, waiting for transfers between devices, flip(): return lax.ppermute(value, axis, [(i, i ^ bit) for i in range(size)])  53.6 us
    pallas_call x2, Pallas kernels, attend_back(): pl.pallas_call(functools.partial(attend_back_body, heads, piece, len(kvs)...  41.1 us
    pallas_call x2, Pallas kernels, attend(): pl.pallas_call(functools.partial(attend_body, heads, piece, len(kvs), car...  36.4 us
    pallas_call x1, Pallas kernels, middle_part(): pl.pallas_call(middle_body, grid_spec=pltpu.PrefetchScalarGridSpec(num_sc...  18.8 us
    ppermute x23, starting transfers between devices, flip(): return lax.ppermute(value, axis, [(i, i ^ bit) for i in range(size)])  18.7 us
    all_to_all x4, starting transfers between devices, swap_rows(): return lax.all_to_all(value, 'tp', 0, 0, tiled=True)  17.8 us
    all_to_all x1, blocking collectives, swap_rows(): return lax.all_to_all(value, 'tp', 0, 0, tiled=True)  14.8 us
  transfers between devices with their start and end apart: 30, of which 18 were waited for; matrix products, arithmetic and copies ran while one was open for 14% of the time, Pallas kernels for 23%

commit v1 on v0

--- a/solution.py
+++ b/solution.py
@@ -392,10 +392,10 @@
     return value
 
 
-def reduce_projections(grad, dps):
+def reduce_projections(grad, late, dps):
     if dps != 2:
         grad = lax.psum_scatter(grad, ("dp", "y", "core"), scatter_dimension=0, tiled=True)
-        return lax.all_gather(grad, ("y", "core"), axis=0, tiled=True)
+        return lax.all_gather(grad, ("y", "core"), axis=0, tiled=True), late
     dp, y, core = lax.axis_index("dp"), lax.axis_index("y"), lax.axis_index("core")
     size = grad.shape[0] // 8
     grad = grad.reshape(2, 2, 2 * size, -1)
@@ -404,7 +404,8 @@
     grad = add_low(pick(grad, dp, 0), flip(pick(grad, 1 - dp, 0), "dp"))
     grad = grad.reshape(2, size, -1)
     grad = add_low(pick(grad, y, 0), flip(pick(grad, 1 - y, 0), "y"))
-    return pair(pair(grad, "y", 0), "core", 0)
+    grad, late = lax.optimization_barrier((grad, late))
+    return pair(pair(grad, "y", 0), "core", 0), late
 
 
 def join_body(keep_ref, send_ref, keepo_ref, sendo_ref, out_ref):
@@ -582,7 +583,9 @@
     back = dot(dq, qkv_full[:, :local], NT) + lax.dot_general(
         dkv, qkv_full[:, local:], (((0,), (1,)), ((), ())), preferred_element_type=f32
     )
-    back = swap_rows(back.astype(bf16).reshape(tps, rows, model))
+    back = back.astype(bf16).reshape(tps, rows, model)
+    normed = after(normed, back)
+    back = swap_rows(back)
     grad_qkv = jnp.concatenate(
         (
             lax.dot_general(normed, dq, (((0,), (0,)), ((), ())), preferred_element_type=f32),
@@ -590,7 +593,8 @@
         ),
         axis=1,
     ).astype(bf16)
-    grad_qkv = reduce_projections(grad_qkv, dps).astype(f32)
+    grad_qkv, back = reduce_projections(grad_qkv, back, dps)
+    grad_qkv = grad_qkv.astype(f32)
     grad_w_qkv = jnp.stack([grad_qkv[:, i * local : (i + 1) * local] for i in range(3)])
 
     e = jnp.sum(back.astype(f32), axis=0)

time: 352 us -> 349 us (level)
  waiting for transfers between devices: 112 us -> 107 us
    ppermute x23, waiting for transfers between devices: 53.6 us -> 49.2 us  [flip(): return lax.ppermute(value, axis, [(i, i ^ bit) for i in range(size)])]
    unnamed x66 -> x62, local copies, waits for them, and re-layouts: 6.8 us -> 9.05 us
where the time goes in v1:
time: 349 us; the launch traced here: 348 us
  waiting for transfers between devices  107 us (31%)
  Pallas kernels  107 us (31%)
  starting transfers between devices  37.8 us (11%)
  local copies, waits for them, and re-layouts  29.1 us (8%)
  other arithmetic  26.3 us (8%)
  between operations  17 us (5%)
  blocking collectives  14.8 us (4%)
  matrix products  9.43 us (3%)
    all_to_all x4, waiting for transfers between devices, swap_rows(): return lax.all_to_all(value, 'tp', 0, 0, tiled=True)  56.1 us
    ppermute x23, waiting for transfers between devices, flip(): return lax.ppermute(value, axis, [(i, i ^ bit) for i in range(size)])  49.2 us
    pallas_call x2, Pallas kernels, attend_back(): pl.pallas_call(functools.partial(attend_back_body, heads, piece, len(kvs)...  41.2 us
    pallas_call x2, Pallas kernels, attend(): pl.pallas_call(functools.partial(attend_body, heads, piece, len(kvs), car...  36.4 us
    ppermute x23, starting transfers between devices, flip(): return lax.ppermute(value, axis, [(i, i ^ bit) for i in range(size)])  19.7 us
    pallas_call x1, Pallas kernels, middle_part(): pl.pallas_call(middle_body, grid_spec=pltpu.PrefetchScalarGridSpec(num_sc...  18.8 us
    all_to_all x4, starting transfers between devices, swap_rows(): return lax.all_to_all(value, 'tp', 0, 0, tiled=True)  17.9 us
    all_to_all x1, blocking collectives, swap_rows(): return lax.all_to_all(value, 'tp', 0, 0, tiled=True)  14.8 us
  transfers between devices with their start and end apart: 30, of which 18 were waited for; matrix products, arithmetic and copies ran while one was open for 14% of the time, Pallas kernels for 23%

profile of v1, /device:TPU:0, one launch (start us, length us, event | category | flops | bytes accessed | tf_op | source)
XLA Modules:
  0.0 347.9 jit_solution(1943693904595045573)
XLA Ops:
  8.3 1.1 constant_dynamic-slice_fusion.3
  12.5 3.0 collective-permute-start
  19.2 2.1 collective-permute-start.1
  21.3 7.8 %collective-permute-done.1 = bf16[8,384]{1,0:T(8,128)(2,1)S(1)} collective-permute-done((bf16[8,384]{1,0:T(8,128)(2,1)S(1)}, bf16[8,384]{1,0:T(8,128)(2,1)S(1)}, u32[]{:S(2)}, u32[]{:S(2)}) %collective-permute-start.1) | collective-permute-done | bytes 6176 | tf_op jit(solution)/shard_map/ppermute | solution.py:350
  31.5 1.5 broadcast_select_fusion.1
  35.3 1.1 collective-permute-start.3
  36.4 2.8 fusion.3.q_ref
  40.2 16.1 %attend.2 = (f32[1024,192]{1,0:T(8,128)}, f32[1024,128]{1,0:T(8,128)}) custom-call(bf16[1024,192]{1,0:T(8,128)(2,1)} %fusion.3.q_ref, bf16[384,1024]{1,0:T(8,128)(2,1)} %copy-done.26, bf16[384,1024]{1,0:T(8,128)(2,1)} %copy-done.27, f32[1,1024]{1,0:T(1,128)} %get-tuple-element.154.refs_2_, f32[1,1024]{1,0:T(1,128)} %get-tuple-element.153.refs_3_), custom_call_target="tpu_custom_call" | custom-call | flops 6442450944 | bytes 2752512 | tf_op jit(solution)/shard_map/attend/pallas_call | solution.py:97
  56.3 3.9 %collective-permute-done.3.refs_0_ = bf16[384,1024]{1,0:T(8,128)(2,1)} collective-permute-done((bf16[384,1024]{1,0:T(8,128)(2,1)S(1)}, bf16[384,1024]{1,0:T(8,128)(2,1)}, u32[]{:S(2)}, u32[]{:S(2)}) %collective-permute-start.3) | collective-permute-done | bytes 786464 | tf_op jit(solution)/shard_map/ppermute | solution.py:350
  60.8 1.9 collective-permute-done.5.refs_1_
  63.6 20.3 %attend.3 = (f32[1024,192]{1,0:T(8,128)}, f32[1024,128]{1,0:T(8,128)}, bf16[1024,192]{1,0:T(8,128)(2,1)}) custom-call(bf16[1024,192]{1,0:T(8,128)(2,1)} %fusion.3.q_ref, bf16[384,1024]{1,0:T(8,128)(2,1)} %collective-permute-done.3.refs_0_, bf16[384,1024]{1,0:T(8,128)(2,1)} %copy-done.28, f32[1,1024]{1,0:T(1,128)} %get-tuple-element.152.refs_2_, ...), custom_call_target="tpu_custom_call" | custom-call | flops 6442450944 | bytes 2752512 | tf_op jit(solution)/shard_map/attend/pallas_call | solution.py:97
  83.9 2.0 copy.37
  85.9 5.4 %all-to-all-start = ((bf16[4,256,192]{1,2,0:T(8,128)(2,1)}), bf16[4,256,192]{1,2,0:T(8,128)(2,1)S(1)}, u32[]{:S(2)}, u32[]{:S(2)}) async-start(bf16[4,256,192]{1,2,0:T(8,128)(2,1)} %copy.37), calls=%async_computation | async-start | bytes 786432 | tf_op jit(solution)/shard_map/all_to_all | solution.py:358
  92.6 19.5 %all-to-all-done = bf16[4,256,192]{1,2,0:T(8,128)(2,1)S(1)} async-done(((bf16[4,256,192]{1,2,0:T(8,128)(2,1)}), bf16[4,256,192]{1,2,0:T(8,128)(2,1)S(1)}, u32[]{:S(2)}, u32[]{:S(2)}) %all-to-all-start) | async-done | bytes 393248 | tf_op jit(solution)/shard_map/all_to_all | solution.py:358
  112.1 1.0 copy.41.att_ref
  113.1 1.5 all-gather.2.cloned.1.call-done
  114.6 18.8 %middle.1 = (bf16[256,768]{1,0:T(8,128)(2,1)}, f32[256,768]{1,0:T(8,128)}, bf16[4,256,192]{2,1,0:T(8,128)(2,1)}, bf16[4,4,192,768]{3,2,1,0:T(8,128)(2,1)}, bf16[...) custom-call(s32[4]{0:T(128)} %pad_add_fusion.num_ref, ...), custom_call_target="tpu_custom_call" | custom-call | flops 7247757312 | bytes 22020096 | tf_op jit(solution)/shard_map/middle/pallas_call | solution.py:293
  134.0 1.2 copy.42
  135.2 14.8 %all_to_all.25 = bf16[4,256,192]{1,2,0:T(8,128)(2,1)S(1)} all-to-all(bf16[4,256,192]{1,2,0:T(8,128)(2,1)S(1)} %copy.42), channel_id=1, replica_groups=mesh['dp'=2,'y'=2,'core'=2,'tp'=4] {'tp'}, dimensions={0} | all-to-all | bytes 786432 | tf_op jit(solution)/shard_map/all_to_all | solution.py:358
  150.0 1.0 copy.43
  151.9 7.1 %join.1 = bf16[4,4,192,896]{3,2,1,0:T(8,128)(2,1)} custom-call(bf16[4,4,192,768]{3,2,1,0:T(8,128)(2,1)} %get-tuple-element.57.keep_ref, bf16[4,4,192,768]{3,2,1,0:T(8,128)(2,1)} %collective-permute-done.6.send_ref, bf16[4,4,192,128]{3,2,1,0:T(8,128)(2,1)} %get-tuple-element.59.keepo_ref, bf16[4,4,192,128]{3,2,1,0:T(8,128)(2,1)} %copy-done.15), custom_call_target="tpu_custom_call" | custom-call | flops 2359296 | bytes 16515072 | tf_op jit(solution)/shard_map/join/pallas_call | solution.py:423
  159.9 1.2 broadcast_in_dim.105
  161.2 3.9 %all-to-all-start.2 = ((bf16[4,256,768]{2,1,0:T(8,128)(2,1)}), bf16[4,256,768]{2,1,0:T(8,128)(2,1)S(1)}, u32[]{:S(2)}, u32[]{:S(2)}) async-start(bf16[4,256,768]{2,1,0:T(8,128)(2,1)} %broadcast_in_dim.105), calls=%async_computation.2 | async-start | bytes 3145728 | tf_op jit(solution)/shard_map/all_to_all | solution.py:358
  165.1 20.4 %attend_back.2 = (f32[1024,192]{1,0:T(8,128)}, bf16[384,1024]{1,0:T(8,128)(2,1)}, bf16[384,1024]{1,0:T(8,128)(2,1)}) custom-call(bf16[1024,192]{1,0:T(8,128)(2,1)} %fusion.3.q_ref, bf16[1024,192]{1,0:T(8,128)(2,1)} %bitcast.95, f32[1024,192]{1,0:T(8,128)} %get-tuple-element.62.att_ref, f32[1024,128]{1,0:T(8,128)} %get-tuple-element.63.log_ref, ...), custom_call_target="tpu_custom_call" | custom-call | flops 1610612736 | bytes 5505024 | tf_op jit(solution)/shard_map/attend_back/pallas_call | solution.py:175
  185.6 2.5 collective-permute-done.8
  188.1 2.3 add_convert_fusion.3
  190.4 1.4 collective-permute-start.10
  191.8 20.8 %attend_back.3 = (bf16[1024,192]{1,0:T(8,128)(2,1)}, bf16[384,1024]{1,0:T(8,128)(2,1)}, bf16[384,1024]{1,0:T(8,128)(2,1)}) custom-call(bf16[1024,192]{1,0:T(8,128)(2,1)} %fusion.3.q_ref, bf16[1024,192]{1,0:T(8,128)(2,1)} %bitcast.96, f32[1024,192]{1,0:T(8,128)} %get-tuple-element.62.att_ref, f32[1024,128]{1,0:T(8,128)} %get-tuple-element.63.log_ref, ...), custom_call_target="tpu_custom_call" | custom-call | flops 1610612736 | bytes 5505024 | tf_op jit(solution)/shard_map/attend_back/pallas_call | solution.py:175
  212.7 5.5 %collective-permute-done.10 = bf16[384,1024]{1,0:T(8,128)(2,1)S(1)} collective-permute-done((bf16[384,1024]{1,0:T(8,128)(2,1)}, bf16[384,1024]{1,0:T(8,128)(2,1)S(1)}, u32[]{:S(2)}, u32[]{:S(2)}) %collective-permute-start.10) | collective-permute-done | bytes 786464 | tf_op jit(solution)/shard_map/ppermute | solution.py:350
  219.0 2.1 add_convert_fusion.2
  221.2 1.0 fusion.24
  222.2 1.7 add_convert_fusion
  223.9 4.7 %all-to-all-start.3 = ((bf16[4,256,768]{2,1,0:T(8,128)(2,1)}), bf16[4,256,768]{2,1,0:T(8,128)(2,1)}, u32[]{:S(2)}, u32[]{:S(2)}) async-start(bf16[4,256,768]{2,1,0:T(8,128)(2,1)} %bitcast.24), calls=%async_computation.3 | async-start | bytes 3145728 | tf_op jit(solution)/shard_map/all_to_all | solution.py:358
  228.8 1.8 convolution_convert_fusion
  230.6 1.2 convolution_convert_fusion.1
  231.9 1.4 concatenate.77
  233.8 2.0 fusion.19
  235.9 2.0 collective-permute-done.11
  237.9 2.1 fusion.4
  240.1 1.0 dynamic-slice_bitcast_fusion
  241.1 1.5 collective-permute-start.12
  242.9 6.3 %collective-permute-done.12 = bf16[192,576]{1,0:T(8,128)(2,1)S(1)} collective-permute-done((bf16[192,576]{1,0:T(8,128)(2,1)S(1)}, bf16[192,576]{1,0:T(8,128)(2,1)S(1)}, u32[]{:S(2)}, u32[]{:S(2)}) %collective-permute-start.12) | collective-permute-done | bytes 221216 | tf_op jit(solution)/shard_map/ppermute | solution.py:350
  249.8 4.4 %collective-permute-done.13 = bf16[96,576]{1,0:T(8,128)(2,1)S(1)} collective-permute-done((bf16[96,576]{1,0:T(8,128)(2,1)S(1)}, bf16[96,576]{1,0:T(8,128)(2,1)S(1)}, u32[]{:S(2)}, u32[]{:S(2)}) %collective-permute-start.13) | collective-permute-done | bytes 110624 | tf_op jit(solution)/shard_map/ppermute | solution.py:350
  254.3 31.5 %all-to-all-done.3 = bf16[4,256,768]{2,1,0:T(8,128)(2,1)} async-done(((bf16[4,256,768]{2,1,0:T(8,128)(2,1)}), bf16[4,256,768]{2,1,0:T(8,128)(2,1)}, u32[]{:S(2)}, u32[]{:S(2)}) %all-to-all-start.3) | async-done | bytes 1572896 | tf_op jit(solution)/shard_map/all_to_all | solution.py:358
  285.8 2.2 convert_reduce_fusion
  288.8 1.2 broadcast_in_dim.107
  290.0 3.8 %all-to-all-start.4 = ((bf16[4,256,768]{2,1,0:T(8,128)(2,1)}), bf16[4,256,768]{2,1,0:T(8,128)(2,1)S(1)}, u32[]{:S(2)}, u32[]{:S(2)}) async-start(bf16[4,256,768]{2,1,0:T(8,128)(2,1)} %broadcast_in_dim.107), calls=%async_computation.4 | async-start | bytes 3145728 | tf_op jit(solution)/shard_map/all_to_all | solution.py:358
  294.6 1.4 collective-permute-start.16
  296.1 3.7 %collective-permute-done.21 = bf16[96,576]{1,0:T(8,128)(2,1)S(1)} collective-permute-done((bf16[96,576]{1,0:T(8,128)(2,1)S(1)}, bf16[96,576]{1,0:T(8,128)(2,1)S(1)}, u32[]{:S(2)}, u32[]{:S(2)}) %collective-permute-start.21) | collective-permute-done | bytes 110624 | tf_op jit(solution)/shard_map/ppermute | solution.py:350
  299.9 3.6 %collective-permute-done.16 = bf16[192,896]{1,0:T(8,128)(2,1)S(1)} collective-permute-done((bf16[192,896]{1,0:T(8,128)(2,1)}, bf16[192,896]{1,0:T(8,128)(2,1)S(1)}, u32[]{:S(2)}, u32[]{:S(2)}) %collective-permute-start.16) | collective-permute-done | bytes 344096 | tf_op jit(solution)/shard_map/ppermute | solution.py:350
  303.5 1.0 broadcast_select_fusion.3
  307.4 1.0 broadcast_select_fusion.5
  309.3 3.4 collective-permute-done.15
  312.7 1.5 collective-permute-start.18
  314.4 2.4 collective-permute-done.18
  316.8 1.7 collective-permute-start.19
  318.6 1.1 pad_maximum_fusion
  319.7 2.5 copy.46
  322.2 2.4 collective-permute-start.20
  324.7 5.2 %all-to-all-done.4 = bf16[4,256,768]{2,1,0:T(8,128)(2,1)S(1)} async-done(((bf16[4,256,768]{2,1,0:T(8,128)(2,1)}), bf16[4,256,768]{2,1,0:T(8,128)(2,1)S(1)}, u32[]{:S(2)}, u32[]{:S(2)}) %all-to-all-start.4) | async-done | bytes 1572896 | tf_op jit(solution)/shard_map/all_to_all | solution.py:358
  329.8 1.9 bitcast_convert_fusion
  331.7 3.2 unpack.1
  338.3 1.5 select_add_fusion
  339.7 1.1 copy.59
  (169 shorter events, 27.9 us)
Async XLA Ops:
  7.2 11.4 %copy-start = (bf16[1000,384]{1,0:T(8,128)(2,1)S(1)}, bf16[1000,384]{1,0:T(8,128)(2,1)}, u32[]{:S(2)}) copy-start(bf16[1000,384]{1,0:T(8,128)(2,1)} %param.17) | copy-start | bytes 2304004
  7.2 8.4 %copy-start.18 = (bf16[3,384,192]{1,2,0:T(8,128)(2,1)S(1)}, bf16[3,384,192]{1,2,0:T(8,128)(2,1)}, u32[]{:S(2)}) copy-start(bf16[3,384,192]{1,2,0:T(8,128)(2,1)} %param.20) | copy-start | bytes 1327108
  7.2 107.4 %all-gather.2.cloned.1.call-start = ((), (), s32[]{:S(2)}) async-start(), calls=%async_computation.7 | async-start | bytes 11354112 | tf_op jit(solution)/shard_map/all_gather | solution.py:516
  10.5 8.6 %copy-start.21 = (bf16[2,384]{1,0:T(2,128)(2,1)S(1)}, bf16[2,384]{1,0:T(2,128)(2,1)}, u32[]{:S(2)}) copy-start(bf16[2,384]{1,0:T(2,128)(2,1)} %param.23) | copy-start | bytes 4612
  10.5 8.6 %copy-start.22 = (bf16[2,384]{1,0:T(2,128)(2,1)S(1)}, bf16[2,384]{1,0:T(2,128)(2,1)}, u32[]{:S(2)}) copy-start(bf16[2,384]{1,0:T(2,128)(2,1)} %param.19) | copy-start | bytes 4612
  10.5 8.6 %copy-start.23 = (bf16[2,384]{1,0:T(2,128)(2,1)S(1)}, bf16[2,384]{1,0:T(2,128)(2,1)}, u32[]{:S(2)}) copy-start(bf16[2,384]{1,0:T(2,128)(2,1)} %param.18) | copy-start | bytes 4612
  10.5 10.7 %copy-start.25 = (bf16[2,192]{1,0:T(2,128)(2,1)S(1)}, bf16[2,192]{1,0:T(2,128)(2,1)}, u32[]{:S(2)}) copy-start(bf16[2,192]{1,0:T(2,128)(2,1)} %param.21) | copy-start | bytes 2308
  11.5 18.2 %copy-start.2 = (bf16[1,1024,768]{2,1,0:T(8,128)(2,1)S(1)}, bf16[1,1024,768]{2,1,0:T(8,128)(2,1)}, u32[]{:S(2)}) copy-start(bf16[1,1024,768]{2,1,0:T(8,128)(2,1)} %param.14) | copy-start | bytes 4718596
  12.5 4.7 %collective-permute-start = (s32[1]{0:T(128)}, s32[1]{0:T(128)}, u32[]{:S(2)}, u32[]{:S(2)}) collective-permute-start(s32[1]{0:T(128)} %param.15), channel_id=1, source_target_pairs={{0,16},{16,0},{1,17},{17,1},{2,18},{18,2},{3,19},{19,3},{4,20},{20... | collective-permute-start | bytes 20 | tf_op jit(solution)/shard_map/ppermute | solution.py:350
  15.7 15.9 %collective-permute-start.2 = (bf16[384,576]{0,1:T(8,128)(2,1)S(1)}, bf16[384,576]{0,1:T(8,128)(2,1)}, u32[]{:S(2)}, u32[]{:S(2)}) collective-permute-start(bf16[384,576]{0,1:T(8,128)(2,1)S(1)} %pad_maximum_fusion.3), channel_id=1, source_target_pairs={{0,16},{16,0},{1,17},{17,1},{2,18},{18,2},{3,19},{19,3},{4,20},{20... | collective-permute-start | bytes 1327112 | tf_op jit(solution)/shard_map/ppermute | solution.py:350
  19.2 9.9 %collective-permute-start.1 = (bf16[8,384]{1,0:T(8,128)(2,1)S(1)}, bf16[8,384]{1,0:T(8,128)(2,1)S(1)}, u32[]{:S(2)}, u32[]{:S(2)}) collective-permute-start(bf16[8,384]{1,0:T(8,128)(2,1)S(1)} %pad_maximum_fusion.8), channel_id=1, source_target_pairs={{0,16},{16,0},{1,17},{17,1},{2,18},{18,2},{3,19},{19,3},{4,20},{20... | collective-permute-start | bytes 18440 | tf_op jit(solution)/shard_map/ppermute | solution.py:350
  31.5 2.4 copy-start.13
  33.1 3.4 copy-start.6
  33.9 5.3 %copy-start.26 = (bf16[384,1024]{1,0:T(8,128)(2,1)}, bf16[384,1024]{1,0:T(8,128)(2,1)S(1)}, u32[]{:S(2)}) copy-start(bf16[384,1024]{1,0:T(8,128)(2,1)S(1)} %add_convert_fusion.4.refs_0_) | copy-start | bytes 2359300
  33.9 5.3 %collective-permute-start.4 = (bf16[384,1024]{1,0:T(8,128)(2,1)S(1)}, bf16[384,1024]{1,0:T(8,128)(2,1)S(1)}, u32[]{:S(2)}, u32[]{:S(2)}) collective-permute-start(bf16[384,1024]{1,0:T(8,128)(2,1)S(1)} %add_convert_fusion.4.refs_0_), channel_id=1, source_target_pairs={{0,4},{4,0},{1,5},{5,1},{2,6},{6,2},{3,7},{7,3},{8,12},{12,8},{9,1... | collective-permute-start | bytes 2359304 | tf_op jit(solution)/shard_map/ppermute | solution.py:350
  35.3 24.9 %collective-permute-start.3 = (bf16[384,1024]{1,0:T(8,128)(2,1)S(1)}, bf16[384,1024]{1,0:T(8,128)(2,1)}, u32[]{:S(2)}, u32[]{:S(2)}) collective-permute-start(bf16[384,1024]{1,0:T(8,128)(2,1)S(1)} %add_convert_fusion.4.refs_0_), channel_id=1, source_target_pairs={{0,8},{8,0},{1,9},{9,1},{2,10},{10,2},{3,11},{11,3},{4,12},{12,4},... | collective-permute-start | bytes 2359304 | tf_op jit(solution)/shard_map/ppermute | solution.py:350
  39.3 0.9 copy-start.27
  60.2 2.5 collective-permute-start.5
  62.7 0.9 copy-start.28
  85.9 26.2 %all-to-all-start = ((bf16[4,256,192]{1,2,0:T(8,128)(2,1)}), bf16[4,256,192]{1,2,0:T(8,128)(2,1)S(1)}, u32[]{:S(2)}, u32[]{:S(2)}) async-start(bf16[4,256,192]{1,2,0:T(8,128)(2,1)} %copy.37), calls=%async_computation | async-start | bytes 786432 | tf_op jit(solution)/shard_map/all_to_all | solution.py:358
  91.3 148.8 %reduce-scatter.3.cloned.1.call-start = ((), (), s32[]{:S(2)}) async-start(), calls=%async_computation.8 | async-start | bytes 6881280 | tf_op jit(solution)/shard_map/reduce_scatter | solution.py:566
  133.4 17.6 %collective-permute-start.6 = (bf16[4,4,192,768]{3,2,1,0:T(8,128)(2,1)}, bf16[4,4,192,768]{3,2,1,0:T(8,128)(2,1)}, u32[]{:S(2)}, u32[]{:S(2)}) collective-permute-start(bf16[4,4,192,768]{3,2,1,0:T(8,128)(2,1)} %get-tuple-element.53), channel_id=1, source_target_pairs={{0,4},{4,0},{1,5},{5,1},{2,6},{6,2},{3,7},{7,3},{8,12},{12,8},{9,1... | collective-permute-start | bytes 14155784 | tf_op jit(solution)/shard_map/ppermute | solution.py:350
  133.7 17.3 %collective-permute-start.7 = (bf16[4,4,192,128]{3,2,1,0:T(8,128)(2,1)}, bf16[4,4,192,128]{3,2,1,0:T(8,128)(2,1)S(1)}, u32[]{:S(2)}, u32[]{:S(2)}) collective-permute-start(bf16[4,4,192,128]{3,2,1,0:T(8,128)(2,1)} %get-tuple-element.54), channel_id=1, source_target_pairs={{0,4},{4,0},{1,5},{5,1},{2,6},{6,2},{3,7},{7,3},{8,12},{12,8},{9,1... | collective-permute-start | bytes 2359304 | tf_op jit(solution)/shard_map/ppermute | solution.py:350
  151.0 0.9 copy-start.15
  158.9 1.0 copy-start.19
  161.2 51.4 %all-to-all-start.2 = ((bf16[4,256,768]{2,1,0:T(8,128)(2,1)}), bf16[4,256,768]{2,1,0:T(8,128)(2,1)S(1)}, u32[]{:S(2)}, u32[]{:S(2)}) async-start(bf16[4,256,768]{2,1,0:T(8,128)(2,1)} %broadcast_in_dim.105), calls=%async_computation.2 | async-start | bytes 3145728 | tf_op jit(solution)/shard_map/all_to_all | solution.py:358
  185.5 2.6 collective-permute-start.8
  190.4 27.7 %collective-permute-start.10 = (bf16[384,1024]{1,0:T(8,128)(2,1)}, bf16[384,1024]{1,0:T(8,128)(2,1)S(1)}, u32[]{:S(2)}, u32[]{:S(2)}) collective-permute-start(bf16[384,1024]{1,0:T(8,128)(2,1)} %add_convert_fusion.3), channel_id=1, source_target_pairs={{0,8},{8,0},{1,9},{9,1},{2,10},{10,2},{3,11},{11,3},{4,12},{12,4},... | collective-permute-start | bytes 2359304 | tf_op jit(solution)/shard_map/ppermute | solution.py:350
  212.6 8.5 %copy-start.4 = (bf16[4,256,768]{2,1,0:T(8,128)(2,1)}, bf16[4,256,768]{2,1,0:T(8,128)(2,1)S(1)}, u32[]{:S(2)}) copy-start(bf16[4,256,768]{2,1,0:T(8,128)(2,1)S(1)} %all-to-all-done.2) | copy-start | bytes 4718596
  212.6 5.6 %collective-permute-start.9 = (bf16[384,1024]{1,0:T(8,128)(2,1)}, bf16[384,1024]{1,0:T(8,128)(2,1)}, u32[]{:S(2)}, u32[]{:S(2)}) collective-permute-start(bf16[384,1024]{1,0:T(8,128)(2,1)} %get-tuple-element.75), channel_id=1, source_target_pairs={{0,4},{4,0},{1,5},{5,1},{2,6},{6,2},{3,7},{7,3},{8,12},{12,8},{9,1... | collective-permute-start | bytes 2359304 | tf_op jit(solution)/shard_map/ppermute | solution.py:350
  218.1 0.9 copy-start.17
  219.0 2.1 copy-start.7
  221.1 1.0 copy-start.9
  223.9 4.9 %copy-start.14 = (bf16[1024,768]{1,0:T(8,128)(2,1)S(1)}, bf16[1024,768]{1,0:T(8,128)(2,1)}, u32[]{:S(2)}) copy-start(bf16[1024,768]{1,0:T(8,128)(2,1)} %copy-done.13) | copy-start | bytes 4718596
  223.9 61.8 %all-to-all-start.3 = ((bf16[4,256,768]{2,1,0:T(8,128)(2,1)}), bf16[4,256,768]{2,1,0:T(8,128)(2,1)}, u32[]{:S(2)}, u32[]{:S(2)}) async-start(bf16[4,256,768]{2,1,0:T(8,128)(2,1)} %bitcast.24), calls=%async_computation.3 | async-start | bytes 3145728 | tf_op jit(solution)/shard_map/all_to_all | solution.py:358
  228.6 2.0 copy-start.10
  228.6 65.9 %reduce-scatter.5.cloned.1.call-start = ((), (), s32[]{:S(2)}) async-start(), calls=%async_computation.9 | async-start | bytes 1720320 | tf_op jit(solution)/shard_map/reduce_scatter | solution.py:567
  231.9 3.9 %copy-start.3 = (bf16[1,1024,768]{2,1,0:T(8,128)(2,1)S(1)}, bf16[1,1024,768]{2,1,0:T(8,128)(2,1)}, u32[]{:S(2)}) copy-start(bf16[1,1024,768]{2,1,0:T(8,128)(2,1)} %param.14) | copy-start | bytes 4718596
  235.7 2.2 collective-permute-start.11
  240.1 9.1 %copy-start.12 = (bf16[2,192,576]{2,1,0:T(8,128)(2,1)S(1)}, bf16[2,192,576]{2,1,0:T(8,128)(2,1)}, u32[]{:S(2)}) copy-start(bf16[2,192,576]{2,1,0:T(8,128)(2,1)} %fusion.4) | copy-start | bytes 1327108
  241.1 8.1 %collective-permute-start.12 = (bf16[192,576]{1,0:T(8,128)(2,1)S(1)}, bf16[192,576]{1,0:T(8,128)(2,1)S(1)}, u32[]{:S(2)}, u32[]{:S(2)}) collective-permute-start(bf16[192,576]{1,0:T(8,128)(2,1)S(1)} %dynamic-slice_bitcast_fusion), channel_id=1, source_target_pairs={{0,16},{16,0},{1,17},{17,1},{2,18},{18,2},{3,19},{19,3},{4,20},{20... | collective-permute-start | bytes 663560 | tf_op jit(solution)/shard_map/ppermute | solution.py:350
  249.3 4.9 %collective-permute-start.13 = (bf16[96,576]{1,0:T(8,128)(2,1)S(1)}, bf16[96,576]{1,0:T(8,128)(2,1)S(1)}, u32[]{:S(2)}, u32[]{:S(2)}) collective-permute-start(bf16[96,576]{1,0:T(8,128)(2,1)S(1)} %dynamic-slice_bitcast_fusion.1), channel_id=1, source_target_pairs={{0,8},{8,0},{1,9},{9,1},{2,10},{10,2},{3,11},{11,3},{4,12},{12,4},... | collective-permute-start | bytes 331784 | tf_op jit(solution)/shard_map/ppermute | solution.py:350
  285.8 2.6 copy-start.16
  290.0 3.8 %copy-start.24 = (f32[8,768]{1,0:T(8,128)S(1)}, f32[8,768]{1,0:T(8,128)}, u32[]{:S(2)}) copy-start(f32[8,768]{1,0:T(8,128)} %get-tuple-element.78) | copy-start | bytes 73732
  290.0 6.0 %copy-start.11 = (bf16[1024,192]{1,0:T(8,128)(2,1)S(1)}, bf16[1024,192]{1,0:T(8,128)(2,1)}, u32[]{:S(2)}) copy-start(bf16[1024,192]{1,0:T(8,128)(2,1)} %get-tuple-element.73) | copy-start | bytes 1179652
  290.0 39.8 %all-to-all-start.4 = ((bf16[4,256,768]{2,1,0:T(8,128)(2,1)}), bf16[4,256,768]{2,1,0:T(8,128)(2,1)S(1)}, u32[]{:S(2)}, u32[]{:S(2)}) async-start(bf16[4,256,768]{2,1,0:T(8,128)(2,1)} %broadcast_in_dim.107), calls=%async_computation.4 | async-start | bytes 3145728 | tf_op jit(solution)/shard_map/all_to_all | solution.py:358
  293.9 6.0 %collective-permute-start.21 = (bf16[96,576]{1,0:T(8,128)(2,1)S(1)}, bf16[96,576]{1,0:T(8,128)(2,1)S(1)}, u32[]{:S(2)}, u32[]{:S(2)}) collective-permute-start(bf16[96,576]{1,0:T(8,128)(2,1)S(1)} %fusion.23), channel_id=1, source_target_pairs={{0,8},{8,0},{1,9},{9,1},{2,10},{10,2},{3,11},{11,3},{4,12},{12,4},... | collective-permute-start | bytes 331784 | tf_op jit(solution)/shard_map/ppermute | solution.py:350
  294.6 9.0 %collective-permute-start.16 = (bf16[192,896]{1,0:T(8,128)(2,1)}, bf16[192,896]{1,0:T(8,128)(2,1)S(1)}, u32[]{:S(2)}, u32[]{:S(2)}) collective-permute-start(bf16[192,896]{1,0:T(8,128)(2,1)} %reduce-scatter.5.cloned.1.call-done), channel_id=1, source_target_pairs={{0,8},{8,0},{1,9},{9,1},{2,10},{10,2},{3,11},{11,3},{4,12},{12,4},... | collective-permute-start | bytes 1032200 | tf_op jit(solution)/shard_map/ppermute | solution.py:350
  299.9 6.4 %copy-start.20 = (f32[4,768]{1,0:T(4,128)S(1)}, f32[4,768]{1,0:T(4,128)}, u32[]{:S(2)}) copy-start(f32[4,768]{1,0:T(4,128)} %get-tuple-element.79) | copy-start | bytes 36868
  304.7 4.6 %copy-start.8 = (bf16[384,896]{1,0:T(8,128)(2,1)}, bf16[384,896]{1,0:T(8,128)(2,1)S(1)}, u32[]{:S(2)}) copy-start(bf16[384,896]{1,0:T(8,128)(2,1)S(1)} %pad_maximum_fusion.1.mine_ref) | copy-start | bytes 2064388
  304.7 8.0 %collective-permute-start.17 = (bf16[384,896]{1,0:T(8,128)(2,1)S(1)}, bf16[384,896]{1,0:T(8,128)(2,1)}, u32[]{:S(2)}, u32[]{:S(2)}) collective-permute-start(bf16[384,896]{1,0:T(8,128)(2,1)S(1)} %pad_maximum_fusion.1.mine_ref), channel_id=1, source_target_pairs={{0,4},{4,0},{1,5},{5,1},{2,6},{6,2},{3,7},{7,3},{8,12},{12,8},{9,1... | collective-permute-start | bytes 2064392 | tf_op jit(solution)/shard_map/ppermute | solution.py:350
  305.6 1.9 collective-permute-start.22
  306.4 2.1 collective-permute-start.14
  308.5 4.2 %collective-permute-start.15 = (f32[14,768]{1,0:T(8,128)S(1)}, f32[14,768]{1,0:T(8,128)S(1)}, u32[]{:S(2)}, u32[]{:S(2)}) collective-permute-start(f32[14,768]{1,0:T(8,128)S(1)} %add.291), channel_id=1, source_target_pairs={{0,8},{8,0},{1,9},{9,1},{2,10},{10,2},{3,11},{11,3},{4,12},{12,4},... | collective-permute-start | bytes 129032 | tf_op jit(solution)/shard_map/ppermute | solution.py:350
  312.7 4.2 %collective-permute-start.18 = (f32[14,768]{1,0:T(8,128)S(1)}, f32[14,768]{1,0:T(8,128)S(1)}, u32[]{:S(2)}, u32[]{:S(2)}) collective-permute-start(f32[14,768]{1,0:T(8,128)S(1)} %add.292), channel_id=1, source_target_pairs={{0,16},{16,0},{1,17},{17,1},{2,18},{18,2},{3,19},{19,3},{4,20},{20... | collective-permute-start | bytes 129032 | tf_op jit(solution)/shard_map/ppermute | solution.py:350
  316.8 5.4 %collective-permute-start.19 = (f32[14,768]{1,0:T(8,128)S(1)}, f32[14,768]{1,0:T(8,128)S(1)}, u32[]{:S(2)}, u32[]{:S(2)}) collective-permute-start(f32[14,768]{1,0:T(8,128)S(1)} %add.293), channel_id=1, source_target_pairs={{0,1},{1,0},{2,3},{3,2},{4,5},{5,4},{6,7},{7,6},{8,9},{9,8},{10,11... | collective-permute-start | bytes 129032 | tf_op jit(solution)/shard_map/ppermute | solution.py:350
  322.2 12.7 %collective-permute-start.20 = (f32[14,768]{1,0:T(8,128)S(1)}, f32[14,768]{1,0:T(8,128)S(1)}, u32[]{:S(2)}, u32[]{:S(2)}) collective-permute-start(f32[14,768]{1,0:T(8,128)S(1)} %add.294), channel_id=1, source_target_pairs={{0,2},{1,3},{2,0},{3,1},{4,6},{5,7},{6,4},{7,5},{8,10},{9,11},{10,... | collective-permute-start | bytes 129032 | tf_op jit(solution)/shard_map/ppermute | solution.py:350
  331.7 8.0 %copy-start.5 = (bf16[4,256,768]{2,1,0:T(8,128)(2,1)S(1)}, bf16[4,256,768]{2,1,0:T(8,128)(2,1)}, u32[]{:S(2)}) copy-start(bf16[4,256,768]{2,1,0:T(8,128)(2,1)} %copy-done.4) | copy-start | bytes 4718596
  339.7 1.6 copy-start.1
Sparse Core Ops, SparseCore 0:
  12.7 101.9 all-gather.1
  159.1 69.4 reduce-scatter.2
  240.2 46.6 reduce-scatter.4
